TPU v7x, 32 devices: a whole 2x2x4 slice. The times are simulated.
32 devices in a mesh: fsdp: 16 (over z, y, core), tp: 2 (over x).
Axes of the slice: x: 2, y: 2, z: 4, core: 2. Of those that a mesh axis runs over, the one named last changes fastest.
Arguments:
- tokens_in: bfloat16 [4096, 2048], P(('fsdp', 'tp')), may hold values from -6 to 6
- cotangent: bfloat16 [4096, 2048], P(('fsdp', 'tp')), may hold values from -6 to 6
- w_query: bfloat16 [2048, 2048], P('fsdp', 'tp'), may hold values from -0.125 to 0.125
- w_key: bfloat16 [2048, 2048], P('fsdp', 'tp'), may hold values from -0.125 to 0.125
- w_value: bfloat16 [2048, 2048], P('fsdp', 'tp'), may hold values from -0.125 to 0.125
- w_output: bfloat16 [2048, 2048], P('tp', 'fsdp'), may hold values from -1 to 1
- gain_query: bfloat16 [16, 128], P('tp', 'fsdp'), may hold values from 0.25 to 1.75
- gain_key: bfloat16 [16, 128], P('tp', 'fsdp'), may hold values from 0.25 to 1.75
- gain_attn: bfloat16 [2048], P('fsdp'), may hold values from 0.25 to 1.75
- gain_moe: bfloat16 [2048], P('fsdp'), may hold values from 0.25 to 1.75
- w_router: bfloat16 [2048, 16], P('fsdp'), may hold values from -0.0625 to 0.0625
- w_gate: bfloat16 [16, 2048, 1024], P('fsdp', None, 'tp'), may hold values from -0.125 to 0.125
- w_up: bfloat16 [16, 2048, 1024], P('fsdp', None, 'tp'), may hold values from -0.125 to 0.125
- w_down: bfloat16 [16, 1024, 2048], P('fsdp', 'tp'), may hold values from -0.75 to 0.75
- expert_ids: int32 [4096, 8], P('fsdp'), may hold values from 0 to 15, all different within a row; in each aligned block of 256 rows (0 to 255, 256 to 511, ...) at most 152 rows name the same one
Outputs:
- block_out: float32 [4096, 2048], P(('fsdp', 'tp'))
- grad_tokens: float32 [4096, 2048], P(('fsdp', 'tp'))
- grad_query: float32 [2048, 2048], P('fsdp', 'tp')
- grad_key: float32 [2048, 2048], P('fsdp', 'tp')
- grad_value: float32 [2048, 2048], P('fsdp', 'tp')
- grad_output: float32 [2048, 2048], P('tp', 'fsdp')
- grad_gain_query: float32 [16, 128], P('tp', 'fsdp')
- grad_gain_key: float32 [16, 128], P('tp', 'fsdp')
- grad_gain_attn: float32 [2048], P('fsdp')
- grad_gain_moe: float32 [2048], P('fsdp')
- grad_router: float32 [2048, 16], P('fsdp')
- grad_gate: float32 [16, 2048, 1024], P('fsdp', None, 'tp')
- grad_up: float32 [16, 2048, 1024], P('fsdp', None, 'tp')
- grad_down: float32 [16, 1024, 2048], P('fsdp', 'tp')
Inputs may be any that keep to these rules, and one draw needn't show every extreme that they name: `expert_ids`: each row names 8 different experts. In each aligned block of 256 rows (one group) no expert is named by more than 152 rows, a bound that some block reaches.
All inputs are finite; a program needn't handle non-finite values.
Results may differ from a plain program's by a relative error of at most 0.018.
Values may be sent and summed in bfloat16 or wider, within the bound.
No kernel may reach another device: no remote copies, remote signals or barrier semaphores. Data moves between devices by JAX's collectives and lax.ppermute only.
A program may use at most 256 MiB of HBM per device.

v0:
```python
import jax
import jax.numpy as jnp
from jax import lax
from jax.sharding import PartitionSpec as P

HEAD = 128
PROMPT = 128
CONT_LEN = 64


epsilon = 1e-05
theta_base = 10000.0
masked_score = -1e30


def rms_scale(values):
    return lax.rsqrt(jnp.mean(values * values, axis=-1, keepdims=True) + epsilon)


def rotate_half(values):
    middle = values.shape[-1] // 2
    return jnp.concatenate([-values[..., middle:], values[..., :middle]], axis=-1)


def rotate_back(values):
    middle = values.shape[-1] // 2
    return jnp.concatenate([values[..., middle:], -values[..., :middle]], axis=-1)


def positions_of(group_len):
    row_index = jnp.arange(group_len, dtype=jnp.int32)
    return jnp.where(row_index < PROMPT, row_index, PROMPT + (row_index - PROMPT) % CONT_LEN)


def attend_mask(group_len):
    row_index = jnp.arange(group_len, dtype=jnp.int32)
    query_pos = row_index[:, None]
    key_pos = row_index[None, :]
    query_cont = (query_pos - PROMPT) // CONT_LEN
    key_cont = (key_pos - PROMPT) // CONT_LEN
    return (key_pos <= query_pos) & ((key_pos < PROMPT) | (query_cont == key_cont))


def rotary_tables(group_len):
    where_pos = positions_of(group_len).astype(jnp.float32)
    frequency = theta_base ** (-2.0 * jnp.arange(HEAD // 2, dtype=jnp.float32) / HEAD)
    angles = where_pos[:, None] * frequency[None, :]
    angles = jnp.concatenate([angles, angles], axis=1)
    return (jnp.cos(angles), jnp.sin(angles))


def rounded(values):
    return lax.optimization_barrier(values.astype(jnp.bfloat16)).astype(jnp.float32)


def head_sums(first, second):
    return lax.psum((first, second), "tp")


def send_slots(block):
    return lax.all_to_all(block, "fsdp", split_axis=0, concat_axis=0, tiled=True)


def return_slots(block):
    return lax.all_to_all(block, "fsdp", split_axis=0, concat_axis=0, tiled=True)


def body(
    tokens_in,
    cotangent,
    w_query,
    w_key,
    w_value,
    w_output,
    gain_query,
    gain_key,
    gain_attn,
    gain_moe,
    w_router,
    w_gate,
    w_up,
    w_down,
    expert_ids,
):
    fsdp_count = lax.axis_size("fsdp")
    part_index = lax.axis_index("tp")
    own_rows = tokens_in.shape[0]
    start_row = part_index * own_rows

    def gather_params():
        return (
            lax.all_gather(w_query, "fsdp", axis=0, tiled=True),
            lax.all_gather(w_key, "fsdp", axis=0, tiled=True),
            lax.all_gather(w_value, "fsdp", axis=0, tiled=True),
            lax.all_gather(w_output, "fsdp", axis=1, tiled=True),
            lax.all_gather(gain_query, "fsdp", axis=1, tiled=True),
            lax.all_gather(gain_key, "fsdp", axis=1, tiled=True),
            lax.all_gather(gain_attn, "fsdp", axis=0, tiled=True),
            lax.all_gather(gain_moe, "fsdp", axis=0, tiled=True),
            lax.all_gather(w_router, "fsdp", axis=0, tiled=True),
        )

    (
        query_mat,
        key_mat,
        value_mat,
        output_mat,
        query_gain,
        key_gain,
        attn_gain,
        moe_gain,
        router_mat,
    ) = gather_params()
    rows_all, grad_rows = (
        lax.all_gather(tokens_in, "tp", axis=0, tiled=True),
        lax.all_gather(cotangent, "tp", axis=0, tiled=True),
    )
    group_len = rows_all.shape[0]
    model_width = rows_all.shape[1]
    topk_count = expert_ids.shape[1]
    expert_count = router_mat.shape[1]
    local_experts = w_gate.shape[0]
    capacity = (group_len * topk_count * 7 // (6 * expert_count) + 7) // 8 * 8
    slot_count = expert_count * capacity
    residual_in = rows_all.astype(jnp.float32)
    scale_one = rms_scale(residual_in)
    normal_one = residual_in * scale_one
    normed_one = (normal_one * attn_gain.astype(jnp.float32)).astype(jnp.bfloat16)
    query_raw = jnp.dot(normed_one, query_mat, preferred_element_type=jnp.float32)
    key_raw = jnp.dot(normed_one, key_mat, preferred_element_type=jnp.float32)
    value_flat = jnp.dot(normed_one, value_mat, preferred_element_type=jnp.float32).astype(
        jnp.bfloat16
    )
    query_sq, key_sq = head_sums(
        jnp.sum(query_raw * query_raw, axis=1), jnp.sum(key_raw * key_raw, axis=1)
    )
    query_scale = lax.rsqrt(query_sq / model_width + epsilon)[:, None]
    key_scale = lax.rsqrt(key_sq / model_width + epsilon)[:, None]
    heads_local = query_gain.shape[0]
    query_gain_flat = query_gain.astype(jnp.float32).reshape(-1)
    key_gain_flat = key_gain.astype(jnp.float32).reshape(-1)
    query_unit = query_raw * query_scale
    key_unit = key_raw * key_scale
    cosine_table, sine_table = rotary_tables(group_len)

    def rotate(matrix):
        pieces = matrix.reshape(group_len, heads_local, HEAD)
        return pieces * cosine_table[:, None, :] + rotate_half(pieces) * sine_table[:, None, :]

    query_rot = rotate(query_unit * query_gain_flat).astype(jnp.bfloat16)
    key_rot = rotate(key_unit * key_gain_flat).astype(jnp.bfloat16)
    value_heads = value_flat.reshape(group_len, heads_local, HEAD)
    allowed = attend_mask(group_len)[None]
    score_scale = HEAD ** (-0.5)

    def scores_now():
        raw_scores = (
            jnp.einsum("qhd,khd->hqk", query_rot, key_rot, preferred_element_type=jnp.float32)
            * score_scale
        )
        return jnp.where(allowed, raw_scores, masked_score)

    scores = scores_now()
    row_top = jnp.max(scores, axis=-1, keepdims=True)
    exp_scores = jnp.exp(scores - row_top)
    exp_total = jnp.sum(exp_scores, axis=-1, keepdims=True)
    log_total = row_top + jnp.log(exp_total)
    context = jnp.einsum(
        "hqk,khd->qhd",
        (exp_scores / exp_total).astype(jnp.bfloat16),
        value_heads,
        preferred_element_type=jnp.float32,
    )
    context_flat = context.reshape(group_len, -1).astype(jnp.bfloat16)
    attn_out = lax.psum(jnp.dot(context_flat, output_mat, preferred_element_type=jnp.float32), "tp")
    hidden = residual_in + attn_out
    scale_two = rms_scale(hidden)
    normal_two = hidden * scale_two
    normed_two = (normal_two * moe_gain.astype(jnp.float32)).astype(jnp.bfloat16)
    logits = jnp.dot(normed_two, router_mat, preferred_element_type=jnp.float32)
    onehot = expert_ids[:, :, None] == jnp.arange(expert_count, dtype=jnp.int32)[None, None, :]
    chosen = jnp.sum(jnp.where(onehot, logits[:, None, :], 0.0), axis=2)
    gate_probs = jax.nn.softmax(chosen, axis=-1)
    per_token = jnp.sum(onehot.astype(jnp.float32), axis=1)
    row_index = jnp.arange(group_len, dtype=jnp.int32)
    earlier = (row_index[None, :] < row_index[:, None]).astype(jnp.float32)
    before = jnp.dot(earlier, per_token, preferred_element_type=jnp.float32)
    slot_index = jnp.sum(jnp.where(onehot, before[:, None, :], 0.0), axis=2).astype(jnp.int32)
    slot_dest = expert_ids * capacity + slot_index
    flat_dest = slot_dest.reshape(-1)
    token_of_slot = (
        jnp.full((slot_count,), group_len, jnp.int32)
        .at[flat_dest]
        .set(jnp.repeat(row_index, topk_count))
    )
    gate_of_slot = jnp.zeros((slot_count,), jnp.float32).at[flat_dest].set(gate_probs.reshape(-1))
    slot_mine = slot_index >= 0
    normed_pad = jnp.concatenate([normed_two, jnp.zeros((1, model_width), jnp.bfloat16)], axis=0)
    cotangent_pad = jnp.concatenate([grad_rows, jnp.zeros((1, model_width), jnp.bfloat16)], axis=0)
    send_shape = (fsdp_count, local_experts, capacity, model_width)
    outgoing = normed_pad[token_of_slot].reshape(send_shape)
    arrived = send_slots(outgoing)
    gate_pre = jnp.einsum("secd,edf->secf", arrived, w_gate, preferred_element_type=jnp.float32)
    up_pre = jnp.einsum("secd,edf->secf", arrived, w_up, preferred_element_type=jnp.float32)
    gate_pre, up_pre, activation = (
        gate_pre,
        up_pre,
        (jax.nn.silu(gate_pre) * up_pre).astype(jnp.bfloat16),
    )
    partial_value = jnp.einsum(
        "secf,efd->secd", activation, w_down, preferred_element_type=jnp.float32
    ).astype(jnp.bfloat16)
    returned = return_slots(partial_value).reshape(-1, model_width)
    cotangent_full = grad_rows.astype(jnp.float32)
    moe_part = jnp.zeros((group_len, model_width), jnp.float32)
    gate_terms = []
    for column in range(topk_count):
        picked = jnp.where(
            slot_mine[:, column : column + 1],
            returned[slot_dest[:, column]].astype(jnp.float32),
            0.0,
        )
        moe_part = moe_part + gate_probs[:, column : column + 1] * picked
        gate_terms.append(jnp.sum(cotangent_full * picked, axis=1))
    moe_own = lax.psum_scatter(
        moe_part.astype(jnp.bfloat16), "tp", scatter_dimension=0, tiled=True
    ).astype(jnp.float32)
    block_out = lax.dynamic_slice_in_dim(hidden, start_row, own_rows, 0) + moe_own
    (
        query_mat,
        key_mat,
        value_mat,
        output_mat,
        query_gain,
        key_gain,
        attn_gain,
        moe_gain,
        router_mat,
    ) = gather_params()
    grad_slot = (
        (cotangent_pad[token_of_slot].astype(jnp.float32) * gate_of_slot[:, None])
        .astype(jnp.bfloat16)
        .reshape(send_shape)
    )
    grad_partial = send_slots(grad_slot)
    grad_act = jnp.einsum(
        "secd,efd->secf", grad_partial, w_down, preferred_element_type=jnp.float32
    )
    grad_down = jnp.einsum(
        "secf,secd->efd", activation, grad_partial, preferred_element_type=jnp.float32
    )
    gate_sig = jax.nn.sigmoid(gate_pre)
    grad_gate_pre = (grad_act * up_pre * gate_sig * (1.0 + gate_pre * (1.0 - gate_sig))).astype(
        jnp.bfloat16
    )
    grad_up_pre = (grad_act * gate_pre * gate_sig).astype(jnp.bfloat16)
    grad_gate = jnp.einsum(
        "secd,secf->edf", arrived, grad_gate_pre, preferred_element_type=jnp.float32
    )
    grad_up = jnp.einsum("secd,secf->edf", arrived, grad_up_pre, preferred_element_type=jnp.float32)
    grad_in = (
        jnp.einsum("secf,edf->secd", grad_gate_pre, w_gate, preferred_element_type=jnp.float32)
        + jnp.einsum("secf,edf->secd", grad_up_pre, w_up, preferred_element_type=jnp.float32)
    ).astype(jnp.bfloat16)
    grad_back = return_slots(grad_in).reshape(-1, model_width)
    grad_normed_part = jnp.zeros((group_len, model_width), jnp.float32)
    for column in range(topk_count):
        grad_normed_part = grad_normed_part + jnp.where(
            slot_mine[:, column : column + 1],
            grad_back[slot_dest[:, column]].astype(jnp.float32),
            0.0,
        )
    grad_normed_moe, grad_gate_probs = lax.psum(
        (grad_normed_part, jnp.stack(gate_terms, axis=1)), "tp"
    )
    grad_chosen = gate_probs * (
        grad_gate_probs - jnp.sum(gate_probs * grad_gate_probs, axis=1, keepdims=True)
    )
    grad_logits = jnp.sum(jnp.where(onehot, grad_chosen[:, :, None], 0.0), axis=1).astype(
        jnp.bfloat16
    )
    grad_router = jnp.einsum(
        "td,te->de", normed_two, grad_logits, preferred_element_type=jnp.float32
    )
    grad_normed_two = grad_normed_moe + jnp.einsum(
        "te,de->td", grad_logits, router_mat, preferred_element_type=jnp.float32
    )
    grad_gain_moe = jnp.sum(grad_normed_two * normal_two, axis=0)
    grad_unit_two = grad_normed_two * moe_gain.astype(jnp.float32)
    grad_hidden = cotangent_full + scale_two * (
        grad_unit_two - normal_two * jnp.mean(grad_unit_two * normal_two, axis=1, keepdims=True)
    )
    grad_attn = grad_hidden.astype(jnp.bfloat16)
    grad_output = jnp.einsum(
        "tc,td->cd", context_flat, grad_attn, preferred_element_type=jnp.float32
    )
    grad_context = (
        jnp.einsum("td,cd->tc", grad_attn, output_mat, preferred_element_type=jnp.float32)
        .astype(jnp.bfloat16)
        .reshape(group_len, heads_local, HEAD)
    )
    attn_probs = jnp.exp(scores_now() - log_total)
    grad_value_rows = (
        jnp.einsum(
            "hqk,qhd->khd",
            attn_probs.astype(jnp.bfloat16),
            grad_context,
            preferred_element_type=jnp.float32,
        )
        .reshape(group_len, -1)
        .astype(jnp.bfloat16)
    )
    grad_probs = jnp.einsum(
        "qhd,khd->hqk", grad_context, value_heads, preferred_element_type=jnp.float32
    )
    grad_scores = (
        attn_probs * (grad_probs - jnp.sum(attn_probs * grad_probs, axis=-1, keepdims=True))
    ).astype(jnp.bfloat16)
    grad_query_rot = rounded(
        jnp.einsum("hqk,khd->qhd", grad_scores, key_rot, preferred_element_type=jnp.float32)
        * score_scale
    )
    grad_key_rot = rounded(
        jnp.einsum("hqk,qhd->khd", grad_scores, query_rot, preferred_element_type=jnp.float32)
        * score_scale
    )

    def unrotate(grad_heads):
        return (
            grad_heads * cosine_table[:, None, :] + rotate_back(grad_heads * sine_table[:, None, :])
        ).reshape(group_len, -1)

    grad_query_norm = unrotate(grad_query_rot)
    grad_key_norm = unrotate(grad_key_rot)
    sum_query, sum_key = head_sums(
        jnp.sum(grad_query_norm * query_gain_flat * query_unit, axis=1),
        jnp.sum(grad_key_norm * key_gain_flat * key_unit, axis=1),
    )
    grad_query_raw = (
        query_scale
        * (query_gain_flat * grad_query_norm - query_unit * (sum_query / model_width)[:, None])
    ).astype(jnp.bfloat16)
    grad_key_raw = (
        key_scale * (key_gain_flat * grad_key_norm - key_unit * (sum_key / model_width)[:, None])
    ).astype(jnp.bfloat16)
    grad_gain_query = jnp.sum(grad_query_norm * query_unit, axis=0).reshape(heads_local, HEAD)
    grad_gain_key = jnp.sum(grad_key_norm * key_unit, axis=0).reshape(heads_local, HEAD)
    grad_query = jnp.einsum(
        "td,tc->dc", normed_one, grad_query_raw, preferred_element_type=jnp.float32
    )
    grad_key = jnp.einsum("td,tc->dc", normed_one, grad_key_raw, preferred_element_type=jnp.float32)
    grad_value = jnp.einsum(
        "td,tc->dc", normed_one, grad_value_rows, preferred_element_type=jnp.float32
    )
    grad_normed_local = (
        jnp.einsum("tc,dc->td", grad_query_raw, query_mat, preferred_element_type=jnp.float32)
        + jnp.einsum("tc,dc->td", grad_key_raw, key_mat, preferred_element_type=jnp.float32)
        + jnp.einsum("tc,dc->td", grad_value_rows, value_mat, preferred_element_type=jnp.float32)
    )
    grad_normed_one = lax.psum(grad_normed_local.astype(jnp.bfloat16), "tp").astype(jnp.float32)
    grad_gain_attn = jnp.sum(grad_normed_one * normal_one, axis=0)
    grad_unit_one = grad_normed_one * attn_gain.astype(jnp.float32)
    grad_full = grad_hidden + scale_one * (
        grad_unit_one - normal_one * jnp.mean(grad_unit_one * normal_one, axis=1, keepdims=True)
    )
    grad_tokens = lax.dynamic_slice_in_dim(grad_full, start_row, own_rows, 0)
    sharded = (
        lax.psum_scatter(grad_query, "fsdp", scatter_dimension=0, tiled=True),
        lax.psum_scatter(grad_key, "fsdp", scatter_dimension=0, tiled=True),
        lax.psum_scatter(grad_value, "fsdp", scatter_dimension=0, tiled=True),
        lax.psum_scatter(grad_output, "fsdp", scatter_dimension=1, tiled=True),
        lax.psum_scatter(grad_gain_query, "fsdp", scatter_dimension=1, tiled=True),
        lax.psum_scatter(grad_gain_key, "fsdp", scatter_dimension=1, tiled=True),
        lax.psum_scatter(grad_gain_attn, "fsdp", scatter_dimension=0, tiled=True),
        lax.psum_scatter(grad_gain_moe, "fsdp", scatter_dimension=0, tiled=True),
        lax.psum_scatter(grad_router, "fsdp", scatter_dimension=0, tiled=True),
    )
    return (
        block_out,
        grad_tokens,
        sharded[0],
        sharded[1],
        sharded[2],
        sharded[3],
        sharded[4],
        sharded[5],
        sharded[6],
        sharded[7],
        sharded[8],
        grad_gate,
        grad_up,
        grad_down,
    )


def solution(mesh):
    in_specs = (
        P(("fsdp", "tp"), None),
        P(("fsdp", "tp"), None),
        P("fsdp", "tp"),
        P("fsdp", "tp"),
        P("fsdp", "tp"),
        P("tp", "fsdp"),
        P("tp", "fsdp"),
        P("tp", "fsdp"),
        P("fsdp"),
        P("fsdp"),
        P("fsdp", None),
        P("fsdp", None, "tp"),
        P("fsdp", None, "tp"),
        P("fsdp", "tp", None),
        P("fsdp", None),
    )
    out_specs = (
        P(("fsdp", "tp"), None),
        P(("fsdp", "tp"), None),
        P("fsdp", "tp"),
        P("fsdp", "tp"),
        P("fsdp", "tp"),
        P("tp", "fsdp"),
        P("tp", "fsdp"),
        P("tp", "fsdp"),
        P("fsdp"),
        P("fsdp"),
        P("fsdp", None),
        P("fsdp", None, "tp"),
        P("fsdp", None, "tp"),
        P("fsdp", "tp", None),
    )
    return jax.shard_map(body, mesh=mesh, in_specs=in_specs, out_specs=out_specs, check_vma=False)
```

profile of v0, /device:TPU:0, one launch (start us, length us, event | category | flops | bytes accessed | tf_op | source)
XLA Modules:
  0.0 2077.5 jit_solution(5803873315009788788)
XLA Ops:
  12.1 23.3 %all-gather = bf16[16,1,128]{2,1,0:T(2,128)(2,1)S(1)} all-gather(bf16[1,1,128]{2,1,0:T(2,128)(2,1)} %bitcast.310), channel_id=1, replica_groups=mesh['fsdp'=16,'tp'=2] {'fsdp'}, dimensions={0}, use_global_device_ids=true | all-gather | bytes 4352 | tf_op jit(solution)/shard_map/all_gather | solution.py:98
  35.4 17.8 all_gather.46
  53.3 18.9 all_gather.44
  74.7 11.6 all-gather.15.cloned.1.call-done
  86.3 4.9 multiply_reduce_fusion.9
  91.1 46.3 %all-gather.13.cloned.1.call-done = bf16[2048,1024]{1,0:T(8,128)(2,1)} async-done(((bf16[128,1024]{1,0:T(8,128)(2,1)}), bf16[2048,1024]{1,0:T(8,128)(2,1)}) %all-gather.13.cloned.1.call-update) | async-done | bytes 4194320 | tf_op jit(solution)/shard_map/all_gather | solution.py:92
  141.9 4.9 all-reduce.8
  162.7 25.7 %all-gather.11.cloned.1.call-done = bf16[2048,1024]{1,0:T(8,128)(2,1)} async-done(((bf16[128,1024]{1,0:T(8,128)(2,1)}), bf16[2048,1024]{1,0:T(8,128)(2,1)}) %all-gather.11.cloned.1.call-update) | async-done | bytes 4194320 | tf_op jit(solution)/shard_map/all_gather | solution.py:94
  194.2 47.2 %all-gather.17.cloned.1.call-done = bf16[1024,2048]{1,0:T(8,128)(2,1)} async-done(((bf16[1024,128]{1,0:T(8,128)(2,1)}), bf16[1024,2048]{1,0:T(8,128)(2,1)}) %all-gather.17.cloned.1.call-update) | async-done | bytes 4194320 | tf_op jit(solution)/shard_map/all_gather | solution.py:95
  241.4 4.9 fusion.108
  247.0 18.5 all-gather.1
  265.7 17.8 all_gather.49
  283.8 24.0 %all-reduce.13.cloned.1.call-done = f32[256,2048]{1,0:T(8,128)} async-done(((f32[256,2048]{1,0:T(8,128)}), f32[256,2048]{1,0:T(8,128)}) %all-reduce.13.cloned.1.call-update) | async-done | bytes 2097168 | tf_op jit(solution)/shard_map/psum | solution.py:175
  311.8 8.5 scatter_custom_fusion
  321.7 10.6 gather_fusion
  332.3 221.4 %all_to_all.20 = bf16[16,1,152,2048]{3,2,1,0:T(8,128)(2,1)S(1)} all-to-all(bf16[16,1,152,2048]{3,2,1,0:T(8,128)(2,1)} %bitcast.256), channel_id=1, replica_groups=mesh['fsdp'=16,'tp'=2] {'fsdp'}, dimensions={0} | all-to-all | bytes 19922944 | tf_op jit(solution)/shard_map/all_to_all | solution.py:61
  553.7 5.6 fusion.12
  559.3 7.8 fusion.19
  568.6 7.7 convert_bitcast_fusion
  576.3 5.9 all-to-all-start.1
  583.0 23.2 %all-gather.19.cloned.1.call-done = bf16[256,2048]{1,0:T(8,128)(2,1)} async-done(((bf16[128,2048]{1,0:T(8,128)(2,1)}), bf16[256,2048]{1,0:T(8,128)(2,1)}) %all-gather.19.cloned.1.call-update) | async-done | bytes 1048592 | tf_op jit(solution)/shard_map/all_gather | solution.py:116
  607.6 10.7 gather_fusion.9
  618.6 141.7 %all-to-all-done.1 = bf16[16,1,152,2048]{3,2,1,0:T(8,128)(2,1)} async-done(((bf16[16,1,152,2048]{3,2,1,0:T(8,128)(2,1)}), bf16[16,1,152,2048]{3,2,1,0:T(8,128)(2,1)}, u32[]{:S(2)}, u32[]{:S(2)}) %all-to-all-start.1) | async-done | bytes 9961504 | tf_op jit(solution)/shard_map/all_to_all | solution.py:65
  760.2 8.5 gather_fusion.8
  768.7 8.4 gather_fusion.7
  777.2 8.5 gather_fusion.6
  785.6 8.7 gather_fusion.5
  794.3 8.5 gather_fusion.4
  802.8 8.5 gather_fusion.3
  811.3 8.5 gather_fusion.2
  819.7 9.0 gather_fusion.1
  828.7 4.9 fusion.50
  833.6 5.1 psum.60
  839.0 8.1 scatter_custom_fusion.1
  847.1 9.3 fusion
  856.4 258.6 %all_to_all.21 = bf16[16,1,152,2048]{3,2,1,0:T(8,128)(2,1)S(1)} all-to-all(bf16[16,1,152,2048]{3,2,1,0:T(8,128)(2,1)} %fusion), channel_id=1, replica_groups=mesh['fsdp'=16,'tp'=2] {'fsdp'}, dimensions={0} | all-to-all | bytes 19922944 | tf_op jit(solution)/shard_map/all_to_all | solution.py:61
  1115.0 14.1 fusion.18
  1129.2 9.6 fusion.37
  1138.7 11.8 fusion.1
  1150.6 221.6 %all_to_all.22 = bf16[16,1,152,2048]{3,2,1,0:T(8,128)(2,1)} all-to-all(bf16[16,1,152,2048]{3,2,1,0:T(8,128)(2,1)} %fusion.1), channel_id=1, replica_groups=mesh['fsdp'=16,'tp'=2] {'fsdp'}, dimensions={0} | all-to-all | bytes 19922944 | tf_op jit(solution)/shard_map/all_to_all | solution.py:65
  1372.2 7.5 gather_fusion.17
  1379.7 7.5 gather_fusion.16
  1387.2 8.5 gather_fusion.15
  1395.6 8.9 gather_fusion.14
  1404.5 8.5 gather_fusion.13
  1413.0 8.4 gather_fusion.12
  1421.4 8.4 gather_fusion.11
  1429.9 8.6 gather_fusion.10
  1438.5 4.7 select_add_fusion
  1444.0 5.6 add_convert_fusion.1
  1449.7 56.9 %all-reduce.15.cloned.1.call-done = f32[256,2048]{1,0:T(8,128)} async-done(((f32[256,2048]{1,0:T(8,128)}), f32[256,2048]{1,0:T(8,128)}) %all-reduce.15.cloned.1.call-update) | async-done | bytes 2097168 | tf_op jit(solution)/shard_map/psum | solution.py:273
  1528.0 5.1 all-reduce.7
  1545.5 6.1 fusion.76
  1552.8 4.6 fusion.98
  1558.4 4.7 fusion.99
  1564.2 4.6 fusion.100
  1574.1 9.9 fusion.24
  1584.0 9.7 fusion.30
  1593.8 7.1 fusion.27
  1604.9 60.0 %all-reduce.6 = (f32[8,128]{1,0:T(8,128)S(1)}, f32[8,128]{1,0:T(8,128)S(1)}, f32[2048]{0:T(1024)S(1)}, f32[2048]{0:T(1024)S(1)}) all-reduce(f32[8,128]{1,0:T(8,128)S(1)} %bitcast.282, f32[8,128]{1,0:T(8,128)S(1)} %bitcast.283, f32[2048]{0:T(1024)S(1)} %get-tuple-element.16, ...), channel_id=7, replica_groups=mesh['fsdp'=16,'tp'=2] {'fsdp'}, use_global_device_ids=true, to_apply=%region_42.43.clone | all-reduce | flops 6144 | bytes 49152
  1670.7 76.8 %reduce-scatter.17.cloned.1.call-done = f32[1024,128]{1,0:T(8,128)} async-done(((f32[1024,2048]{1,0:T(8,128)}), f32[1024,128]{1,0:T(8,128)}) %reduce-scatter.17.cloned.1.call-update) | async-done | bytes 524304 | tf_op jit(solution)/shard_map/reduce_scatter | solution.py:371
  1747.6 107.8 %reduce-scatter.15.cloned.1.call-done = f32[128,1024]{1,0:T(8,128)} async-done(((f32[2048,1024]{1,0:T(8,128)}), f32[128,1024]{1,0:T(8,128)}) %reduce-scatter.15.cloned.1.call-update) | async-done | bytes 524304 | tf_op jit(solution)/shard_map/reduce_scatter | solution.py:370
  1855.3 107.6 %reduce-scatter.13.cloned.1.call-done = f32[128,1024]{1,0:T(8,128)} async-done(((f32[2048,1024]{1,0:T(8,128)}), f32[128,1024]{1,0:T(8,128)}) %reduce-scatter.13.cloned.1.call-update) | async-done | bytes 524304 | tf_op jit(solution)/shard_map/reduce_scatter | solution.py:369
  1963.0 107.6 %reduce-scatter.11.cloned.1.call-done = f32[128,1024]{1,0:T(8,128)} async-done(((f32[2048,1024]{1,0:T(8,128)}), f32[128,1024]{1,0:T(8,128)}) %reduce-scatter.11.cloned.1.call-update) | async-done | bytes 524304 | tf_op jit(solution)/shard_map/reduce_scatter | solution.py:368
  (302 shorter events, 95.0 us)
Async XLA Ops:
  7.2 561.4 %copy-start = (bf16[1,512,2048]{2,1,0:T(8,128)(2,1)S(1)}, bf16[1,512,2048]{2,1,0:T(8,128)(2,1)}, u32[]{:S(2)}) copy-start(bf16[1,512,2048]{2,1,0:T(8,128)(2,1)} %param.28) | copy-start | bytes 6291460
  7.2 65.9 %all-gather.9.cloned.1.call-start = ((), (), s32[]{:S(2)}) async-start(), calls=%async_computation.10 | async-start | bytes 1572864 | tf_op jit(solution)/shard_map/all_gather | solution.py:115
  7.9 78.3 %all-gather.15.cloned.1.call-start = ((), (), s32[]{:S(2)}) async-start(), calls=%async_computation.13 | async-start | bytes 4456448 | tf_op jit(solution)/shard_map/all_gather | solution.py:93
  8.7 128.7 %all-gather.13.cloned.1.call-start = ((), (), s32[]{:S(2)}) async-start(), calls=%async_computation.12 | async-start | bytes 4456448 | tf_op jit(solution)/shard_map/all_gather | solution.py:92
  9.4 179.0 %all-gather.11.cloned.1.call-start = ((), (), s32[]{:S(2)}) async-start(), calls=%async_computation.11 | async-start | bytes 4456448 | tf_op jit(solution)/shard_map/all_gather | solution.py:94
  10.0 231.5 %all-gather.17.cloned.1.call-start = ((), (), s32[]{:S(2)}) async-start(), calls=%async_computation.14 | async-start | bytes 4456448 | tf_op jit(solution)/shard_map/all_gather | solution.py:95
  10.6 297.1 %all-reduce.13.cloned.1.call-start = ((), (), s32[]{:S(2)}) async-start(), calls=%async_computation.15 | async-start | bytes 4194304 | tf_op jit(solution)/shard_map/psum | solution.py:175
  35.4 153.0 %copy-start.34 = (f32[16,1,128]{2,1,0:T(1,128)}, f32[16,1,128]{2,1,0:T(1,128)S(1)}, u32[]{:S(2)}) copy-start(f32[16,1,128]{2,1,0:T(1,128)S(1)} %convert_element_type.290) | copy-start | bytes 24580
  72.9 86.1 %copy-start.30 = (f32[256,128]{0,1:T(8,128)}, f32[256,128]{0,1:T(8,128)S(1)}, u32[]{:S(2)}) copy-start(f32[256,128]{0,1:T(8,128)S(1)} %get-tuple-element.71) | copy-start | bytes 393220
  72.9 86.1 %copy-start.32 = (f32[256,128]{0,1:T(8,128)}, f32[256,128]{0,1:T(8,128)S(1)}, u32[]{:S(2)}) copy-start(f32[256,128]{0,1:T(8,128)S(1)} %get-tuple-element.70) | copy-start | bytes 393220
  72.9 73.9 %copy-start.49 = (f32[1024]{0:T(1024)}, f32[1024]{0:T(1024)S(1)}, u32[]{:S(2)}) copy-start(f32[1024]{0:T(1024)S(1)} %bitcast_convert_fusion) | copy-start | bytes 12292
  72.9 79.3 %copy-start.51 = (f32[1024]{0:T(1024)}, f32[1024]{0:T(1024)S(1)}, u32[]{:S(2)}) copy-start(f32[1024]{0:T(1024)S(1)} %bitcast_convert_fusion.1) | copy-start | bytes 12292
  74.6 113.8 %copy-start.47 = (f32[256]{0:T(256)}, f32[256]{0:T(256)S(1)}, u32[]{:S(2)}) copy-start(f32[256]{0:T(256)S(1)} %add_rsqrt_fusion.3) | copy-start | bytes 3076
  86.3 51.2 %copy-start.2 = (bf16[256,2048]{1,0:T(8,128)(2,1)S(1)}, bf16[256,2048]{1,0:T(8,128)(2,1)}, u32[]{:S(2)}) copy-start(bf16[256,2048]{1,0:T(8,128)(2,1)} %all-gather.9.cloned.1.call-done) | copy-start | bytes 3145732
  152.3 4.9 copy-start.57
  161.1 30.9 %copy-start.45 = (f32[8,256]{1,0:T(8,128)}, f32[8,256]{1,0:T(8,128)S(1)}, u32[]{:S(2)}) copy-start(f32[8,256]{1,0:T(8,128)S(1)} %get-tuple-element.92) | copy-start | bytes 24580
  162.7 29.3 %copy-start.53 = (f32[8,256]{1,0:T(8,128)}, f32[8,256]{1,0:T(8,128)S(1)}, u32[]{:S(2)}) copy-start(f32[8,256]{1,0:T(8,128)S(1)} %fusion.57) | copy-start | bytes 24580
  188.4 4.5 copy-start.5
  246.4 19.3 copy-start.61
  246.4 37.2 %copy-start.43 = (s32[256,8]{0,1:T(8,128)S(1)}, s32[256,8]{0,1:T(8,128)}, u32[]{:S(2)}) copy-start(s32[256,8]{0,1:T(8,128)} %param.29) | copy-start | bytes 24580
  265.6 44.1 %copy-start.41 = (f32[16,1,128]{2,1,0:T(1,128)}, f32[16,1,128]{2,1,0:T(1,128)S(1)}, u32[]{:S(2)}) copy-start(f32[16,1,128]{2,1,0:T(1,128)S(1)} %convert_element_type.291) | copy-start | bytes 24580
  283.6 26.9 %copy-start.37 = (bf16[2048,16]{0,1:T(8,128)(2,1)}, bf16[2048,16]{0,1:T(8,128)(2,1)S(1)}, u32[]{:S(2)}) copy-start(bf16[2048,16]{0,1:T(8,128)(2,1)S(1)} %all_gather.49) | copy-start | bytes 196612
  332.3 221.4 %copy-start.66 = (bf16[1,2048,512]{2,1,0:T(8,128)(2,1)S(1)}, bf16[1,2048,512]{2,1,0:T(8,128)(2,1)}, u32[]{:S(2)}) copy-start(bf16[1,2048,512]{2,1,0:T(8,128)(2,1)} %param.26) | copy-start | bytes 6291460
  553.7 5.6 copy-start.12
  553.7 5.6 copy-start.68
  559.3 7.8 copy-start.77
  576.3 183.9 %all-to-all-start.1 = ((bf16[16,1,152,2048]{3,2,1,0:T(8,128)(2,1)}), bf16[16,1,152,2048]{3,2,1,0:T(8,128)(2,1)}, u32[]{:S(2)}, u32[]{:S(2)}) async-start(bf16[16,1,152,2048]{3,2,1,0:T(8,128)(2,1)} %convert_bitcast_fusion), calls=%async_computation.1 | async-start | bytes 19922944 | tf_op jit(solution)/shard_map/all_to_all | solution.py:65
  582.2 24.0 %all-gather.19.cloned.1.call-start = ((), (), s32[]{:S(2)}) async-start(), calls=%async_computation.17 | async-start | bytes 1572864 | tf_op jit(solution)/shard_map/all_gather | solution.py:116
  583.0 923.7 %all-reduce.15.cloned.1.call-start = ((), (), s32[]{:S(2)}) async-start(), calls=%async_computation.18 | async-start | bytes 4194304 | tf_op jit(solution)/shard_map/psum | solution.py:273
  819.7 9.0 copy-start.14
  1115.0 14.1 copy-start.13
  1115.0 14.1 copy-start.67
  1129.1 9.6 copy-start.75
  1129.1 9.6 copy-start.73
  1129.1 9.6 copy-start.69
  1443.2 128.2 %reduce-scatter.9.cloned.1.call-start = ((), (), s32[]{:S(2)}) async-start(), calls=%async_computation.16 | async-start | bytes 1572864 | tf_op jit(solution)/shard_map/reduce_scatter | solution.py:225
  1444.0 62.7 %copy-start.8 = (f32[256,2048]{1,0:T(8,128)S(1)}, f32[256,2048]{1,0:T(8,128)}, u32[]{:S(2)}) copy-start(f32[256,2048]{1,0:T(8,128)} %copy-done.7) | copy-start | bytes 6291460
  1444.0 62.7 %copy-start.38 = (bf16[2048,16]{0,1:T(8,128)(2,1)S(1)}, bf16[2048,16]{0,1:T(8,128)(2,1)}, u32[]{:S(2)}) copy-start(bf16[2048,16]{0,1:T(8,128)(2,1)} %copy-done.37) | copy-start | bytes 196612
  1444.0 62.7 %copy-start.42 = (f32[16,1,128]{2,1,0:T(1,128)S(1)}, f32[16,1,128]{2,1,0:T(1,128)}, u32[]{:S(2)}) copy-start(f32[16,1,128]{2,1,0:T(1,128)} %copy-done.41) | copy-start | bytes 24580
  1444.0 62.7 %copy-start.60 = (f32[256]{0:T(256)S(1)}, f32[256]{0:T(256)}, u32[]{:S(2)}) copy-start(f32[256]{0:T(256)} %copy-done.59) | copy-start | bytes 3076
  1449.7 151.3 %all-reduce.17.cloned.1.call-start = ((), (), s32[]{:S(2)}) async-start(), calls=%async_computation.19 | async-start | bytes 2097152 | tf_op jit(solution)/shard_map/psum | solution.py:360
  1509.1 3.0 copy-start.65
  1512.0 3.5 copy-start.6
  1512.0 3.5 copy-start.40
  1521.4 4.2 copy-start.52
  1521.4 4.2 copy-start.58
  1523.0 4.6 copy-start.50
  1523.0 4.6 copy-start.56
  1533.2 2.2 copy-start.22
  1535.1 2.6 copy-start.63
  1535.4 3.6 copy-start.19
  1542.1 2.4 copy-start.10
  1544.4 126.4 %reduce-scatter.19.cloned.1.call-start = ((), (), s32[]{:S(2)}) async-start(), calls=%async_computation.24 | async-start | bytes 139264 | tf_op jit(solution)/shard_map/reduce_scatter | solution.py:376
  1545.4 202.2 %reduce-scatter.17.cloned.1.call-start = ((), (), s32[]{:S(2)}) async-start(), calls=%async_computation.23 | async-start | bytes 8912896 | tf_op jit(solution)/shard_map/reduce_scatter | solution.py:371
  1551.6 303.8 %reduce-scatter.15.cloned.1.call-start = ((), (), s32[]{:S(2)}) async-start(), calls=%async_computation.22 | async-start | bytes 8912896 | tf_op jit(solution)/shard_map/reduce_scatter | solution.py:370
  1557.4 405.6 %reduce-scatter.13.cloned.1.call-start = ((), (), s32[]{:S(2)}) async-start(), calls=%async_computation.21 | async-start | bytes 8912896 | tf_op jit(solution)/shard_map/reduce_scatter | solution.py:369
  1563.2 507.4 %reduce-scatter.11.cloned.1.call-start = ((), (), s32[]{:S(2)}) async-start(), calls=%async_computation.20 | async-start | bytes 8912896 | tf_op jit(solution)/shard_map/reduce_scatter | solution.py:368
  1571.4 2.7 copy-start.72
  1574.1 9.9 copy-start.74
  1574.1 19.6 slice-start
  1584.0 9.8 slice-start.1
  1584.0 9.8 slice-start.2
  1584.0 9.8 copy-start.76
  1667.5 403.1 %copy-start.1 = (bf16[1,512,2048]{2,1,0:T(8,128)(2,1)S(1)}, bf16[1,512,2048]{2,1,0:T(8,128)(2,1)}, u32[]{:S(2)}) copy-start(bf16[1,512,2048]{2,1,0:T(8,128)(2,1)} %param.28) | copy-start | bytes 6291460
  (33 other events, 39.3 us)
Sparse Core Ops, SparseCore 0:
  9.5 23.9 all-gather.8
  35.7 50.4 all-gather.14
  88.4 48.9 all-gather.12
  139.4 48.9 all-gather.10
  190.4 51.0 all-gather.16
  246.5 61.1 all-reduce.12
  584.6 21.6 all-gather.18
  1443.4 63.2 all-reduce.14
  1508.9 20.3 reduce-scatter.8
  1544.5 39.9 all-reduce.16
  1588.5 51.8 reduce-scatter.18
  1644.9 102.6 reduce-scatter.16
  1752.2 103.0 reduce-scatter.14
  1859.8 103.0 reduce-scatter.12
  1967.4 103.0 reduce-scatter.10
where the time goes:
time: 2090 us; the launch traced here: 2080 us
  blocking collectives  873 us (42%)
  waiting for transfers between devices  780 us (37%)
  local copies, waits for them, and re-layouts  211 us (10%)
  matrix products  136 us (7%)
  other arithmetic  54 us (3%)
    all_to_all x2, blocking collectives, send_slots(): lax.all_to_all(block, 'fsdp', split_axis=0, concat_axis=0, tiled=True)  480 us
    all_to_all x1, blocking collectives, return_slots(): lax.all_to_all(block, 'fsdp', split_axis=0, concat_axis=0, tiled=True)  222 us
    all_to_all x1, waiting for transfers between devices, return_slots(): lax.all_to_all(block, 'fsdp', split_axis=0, concat_axis=0, tiled=True)  142 us
    reduce_scatter x1, waiting for transfers between devices, body(): lax.psum_scatter(grad_value, 'fsdp', scatter_dimension=0, tiled=True)  108 us
    reduce_scatter x1, waiting for transfers between devices, body(): lax.psum_scatter(grad_key, 'fsdp', scatter_dimension=0, tiled=True)  108 us
    reduce_scatter x1, waiting for transfers between devices, body(): lax.psum_scatter(grad_query, 'fsdp', scatter_dimension=0, tiled=True)  108 us
    reduce_scatter x1, waiting for transfers between devices, body(): lax.psum_scatter(grad_output, 'fsdp', scatter_dimension=1, tiled=True)  76.8 us
    gather x8, local copies, waits for them, and re-layouts, body(): returned[slot_dest[:, column]].astype(jnp.float32)  68.5 us
  transfers between devices with their start and end apart: 16, of which 12 were waited for; matrix products, arithmetic and copies ran while one was open for 6% of the time, Pallas kernels for 0%

commit v1 on v0

--- a/solution.py
+++ b/solution.py
@@ -65,7 +65,7 @@
     return lax.all_to_all(block, "fsdp", split_axis=0, concat_axis=0, tiled=True)
 
 
-def body(
+def sparse_body(
     tokens_in,
     cotangent,
     w_query,
@@ -393,6 +393,327 @@
     )
 
 
+def swap_tp(values):
+    return lax.ppermute(values, "tp", [(0, 1), (1, 0)])
+
+
+def joined_rows(own, other, part_index):
+    first = jnp.where(part_index == 0, own, other)
+    second = jnp.where(part_index == 0, other, own)
+    return jnp.concatenate([first, second], axis=0)
+
+
+def halves_of(values, part_index):
+    rows = values.shape[0] // 2
+    low, high = values[:rows], values[rows:]
+    return jnp.where(part_index == 0, low, high), jnp.where(part_index == 0, high, low)
+
+
+def dense_body(
+    tokens_in,
+    cotangent,
+    w_query,
+    w_key,
+    w_value,
+    w_output,
+    gain_query,
+    gain_key,
+    gain_attn,
+    gain_moe,
+    w_router,
+    w_gate,
+    w_up,
+    w_down,
+    expert_ids,
+):
+    f32, bf16 = jnp.float32, jnp.bfloat16
+    fsdp_count = lax.axis_size("fsdp")
+    part_index = lax.axis_index("tp")
+    expert_index = lax.axis_index("fsdp")
+    own_rows, model_width = tokens_in.shape
+    group_len = 2 * own_rows
+    half_width = w_query.shape[1]
+    topk_count = expert_ids.shape[1]
+    expert_count = w_router.shape[1]
+    shard_rows = w_query.shape[0]
+    heads_local = gain_query.shape[0]
+    gain_cols = gain_query.shape[1]
+    capacity = (group_len * topk_count * 7 // (6 * expert_count) + 7) // 8 * 8
+
+    def dot(left, right, dims):
+        return lax.dot_general(left, right, (dims, ((), ())), preferred_element_type=f32)
+
+    def column(flat):
+        return jnp.pad(flat, (0, shard_rows - flat.shape[0]))[:, None]
+
+    small = jnp.concatenate(
+        [
+            w_router,
+            gain_attn[:, None],
+            gain_moe[:, None],
+            column(gain_query.reshape(-1)),
+            column(gain_key.reshape(-1)),
+        ],
+        axis=1,
+    )
+    small_cols = small.shape[1]
+    small = jnp.pad(small, ((0, 0), (0, 128 - small_cols)))
+    packed = jnp.concatenate([w_query, w_key, w_value, small], axis=1)
+    packed_all = lax.all_gather(packed, "fsdp", axis=0, tiled=True)
+    qkv_mat = packed_all[:, : 3 * half_width]
+    small_all = packed_all[:, 3 * half_width :]
+    router_mat = small_all[:, :expert_count]
+    attn_gain = small_all[:, expert_count].astype(f32)
+    moe_gain = small_all[:, expert_count + 1].astype(f32)
+
+    def head_gain(index):
+        flat = small_all[:, expert_count + 2 + index].reshape(fsdp_count, shard_rows)
+        flat = flat[:, : heads_local * gain_cols].reshape(fsdp_count, heads_local, gain_cols)
+        return jnp.transpose(flat, (1, 0, 2)).reshape(-1).astype(f32)
+
+    query_gain_flat, key_gain_flat = head_gain(0), head_gain(1)
+    out_mat_t = lax.all_gather(w_output.T, "fsdp", axis=0, tiled=True)
+    ids_all = lax.all_gather(expert_ids, "fsdp", axis=0, tiled=True)
+
+    residual_in = joined_rows(tokens_in, swap_tp(tokens_in), part_index).astype(f32)
+    scale_one = rms_scale(residual_in)
+    normed_one = (residual_in * scale_one * attn_gain).astype(bf16)
+    qkv = dot(normed_one, qkv_mat, ((1,), (0,)))
+    query_raw = qkv[:, :half_width]
+    key_raw = qkv[:, half_width : 2 * half_width]
+    value_flat = qkv[:, 2 * half_width :].astype(bf16)
+    squares = jnp.stack(
+        [jnp.sum(query_raw * query_raw, axis=1), jnp.sum(key_raw * key_raw, axis=1)]
+    )
+    squares = squares + swap_tp(squares)
+    query_scale = lax.rsqrt(squares[0] / model_width + epsilon)[:, None]
+    key_scale = lax.rsqrt(squares[1] / model_width + epsilon)[:, None]
+    query_unit = query_raw * query_scale
+    key_unit = key_raw * key_scale
+    cosine_table, sine_table = rotary_tables(group_len)
+
+    def rotate(matrix):
+        pieces = matrix.reshape(group_len, heads_local, HEAD)
+        return pieces * cosine_table[:, None, :] + rotate_half(pieces) * sine_table[:, None, :]
+
+    query_rot = rotate(query_unit * query_gain_flat).astype(bf16)
+    key_rot = rotate(key_unit * key_gain_flat).astype(bf16)
+    value_heads = value_flat.reshape(group_len, heads_local, HEAD)
+    allowed = attend_mask(group_len)[None]
+    score_scale = HEAD ** (-0.5)
+    raw_scores = (
+        jnp.einsum("qhd,khd->hqk", query_rot, key_rot, preferred_element_type=f32) * score_scale
+    )
+    scores = jnp.where(allowed, raw_scores, masked_score)
+    row_top = jnp.max(scores, axis=-1, keepdims=True)
+    exp_scores = jnp.exp(scores - row_top)
+    attn_probs = exp_scores / jnp.sum(exp_scores, axis=-1, keepdims=True)
+    probs_low = attn_probs.astype(bf16)
+    context = jnp.einsum("hqk,khd->qhd", probs_low, value_heads, preferred_element_type=f32)
+    context_flat = context.reshape(group_len, -1).astype(bf16)
+    attn_part = dot(context_flat, out_mat_t, ((1,), (1,)))
+    attn_own, attn_other = halves_of(attn_part, part_index)
+    tokens_own = tokens_in.astype(f32)
+    hidden = tokens_own + (attn_own + swap_tp(attn_other.astype(bf16)).astype(f32))
+    scale_two = rms_scale(hidden)
+    normal_two = hidden * scale_two
+    normed_two = (normal_two * moe_gain).astype(bf16)
+
+    both = ("fsdp", "tp")
+    rows_all = lax.all_gather(normed_two, both, axis=0, tiled=True)
+    cotangent_all = lax.all_gather(cotangent, both, axis=0, tiled=True)
+    expert_row = jnp.arange(expert_count, dtype=jnp.int32)
+
+    def chosen_mask(ids):
+        return jnp.any(ids[:, :, None] == expert_row[None, None, :], axis=1)
+
+    def gates_of(rows, mask):
+        logits = jnp.where(mask, dot(rows, router_mat, ((1,), (0,))), -jnp.inf)
+        top = jnp.max(logits, axis=1, keepdims=True)
+        weights = jnp.where(mask, jnp.exp(logits - top), 0.0)
+        return weights / jnp.sum(weights, axis=1, keepdims=True)
+
+    gates_all = gates_of(rows_all, chosen_mask(ids_all))
+    gate_here = jnp.sum(jnp.where(expert_row[None, :] == expert_index, gates_all, 0.0), axis=1)
+    gate_here = gate_here.reshape(fsdp_count, group_len)
+    named = jnp.any(ids_all == expert_index, axis=1).reshape(fsdp_count, group_len)
+    row_index = jnp.arange(group_len, dtype=jnp.int32)
+    earlier = (row_index[:, None] < row_index[None, :]).astype(bf16)
+    place = dot(named.astype(bf16), earlier, ((1,), (0,))).astype(jnp.int32)
+    slot_row = jnp.arange(capacity, dtype=jnp.int32)
+    select = (slot_row[None, :, None] == place[:, None, :]) & named[:, None, :]
+    select_low = select.astype(bf16)
+    gate_slot = jnp.sum(jnp.where(select, gate_here[:, None, :], 0.0), axis=2)
+
+    def pick(rows):
+        grouped = rows.reshape(fsdp_count, group_len, model_width)
+        return jnp.einsum("gct,gtd->gcd", select_low, grouped, preferred_element_type=f32)
+
+    def spread(slots):
+        return jnp.einsum("gct,gcd->gtd", select_low, slots, preferred_element_type=f32)
+
+    slot_count = fsdp_count * capacity
+    arrived = pick(rows_all).astype(bf16).reshape(slot_count, model_width)
+    gate_mat, up_mat, down_mat = w_gate[0], w_up[0], w_down[0]
+    gate_pre = dot(arrived, gate_mat, ((1,), (0,)))
+    up_pre = dot(arrived, up_mat, ((1,), (0,)))
+    gate_sig = jax.nn.sigmoid(gate_pre)
+    activation = (gate_pre * gate_sig * up_pre).astype(bf16)
+    partial_value = dot(activation, down_mat, ((1,), (0,))).astype(bf16)
+    partial_value = partial_value.reshape(fsdp_count, capacity, model_width)
+    cotangent_slot = pick(cotangent_all)
+    slot_dots = jnp.sum(cotangent_slot * partial_value.astype(f32), axis=2)
+    token_dots = jnp.sum(jnp.where(select, slot_dots[:, :, None], 0.0), axis=1)
+    moe_out = (spread(partial_value) * gate_here[:, :, None]).astype(bf16)
+    moe_out = moe_out.reshape(-1, model_width)
+    dots_owned = lax.all_to_all(token_dots, "fsdp", split_axis=0, concat_axis=0, tiled=True)
+    dots_own, dots_other = halves_of(dots_owned.T, part_index)
+    grad_gates = dots_own + swap_tp(dots_other)
+
+    grad_slot = (cotangent_slot * gate_slot[:, :, None]).astype(bf16)
+    grad_slot = grad_slot.reshape(slot_count, model_width)
+    grad_act = dot(grad_slot, down_mat, ((1,), (1,)))
+    grad_gate_pre = (grad_act * up_pre * gate_sig * (1.0 + gate_pre * (1.0 - gate_sig))).astype(
+        bf16
+    )
+    grad_up_pre = (grad_act * gate_pre * gate_sig).astype(bf16)
+    grad_in = (
+        dot(grad_gate_pre, gate_mat, ((1,), (1,))) + dot(grad_up_pre, up_mat, ((1,), (1,)))
+    ).astype(bf16)
+    grad_rows = spread(grad_in.reshape(fsdp_count, capacity, model_width)).astype(bf16)
+    grad_group = lax.psum_scatter(
+        grad_rows.reshape(-1, model_width), "fsdp", scatter_dimension=0, tiled=True
+    )
+    grad_down = dot(activation, grad_slot, ((0,), (0,)))
+    grad_gate = dot(arrived, grad_gate_pre, ((0,), (0,)))
+    grad_up = dot(arrived, grad_up_pre, ((0,), (0,)))
+
+    def own_sum(group_rows):
+        own, other = halves_of(group_rows, part_index)
+        return own.astype(f32) + swap_tp(other).astype(f32)
+
+    own_ids, _ = halves_of(expert_ids, part_index)
+    gates_own = gates_of(normed_two, chosen_mask(own_ids))
+    grad_logits = (
+        gates_own * (grad_gates - jnp.sum(gates_own * grad_gates, axis=1, keepdims=True))
+    ).astype(bf16)
+    grad_router = dot(normed_two, grad_logits, ((0,), (0,)))
+    grad_normed_two = own_sum(grad_group) + dot(grad_logits, router_mat, ((1,), (1,)))
+    grad_gain_moe = jnp.sum(grad_normed_two * normal_two, axis=0)
+    grad_unit_two = grad_normed_two * moe_gain
+    grad_hidden = cotangent.astype(f32) + scale_two * (
+        grad_unit_two - normal_two * jnp.mean(grad_unit_two * normal_two, axis=1, keepdims=True)
+    )
+    grad_attn_own = grad_hidden.astype(bf16)
+    grad_attn = joined_rows(grad_attn_own, swap_tp(grad_attn_own), part_index)
+
+    grad_output = dot(grad_attn, context_flat, ((0,), (0,)))
+    grad_output = lax.psum_scatter(grad_output.astype(bf16), "fsdp", scatter_dimension=0, tiled=True)
+    moe_group = lax.psum_scatter(moe_out, "fsdp", scatter_dimension=0, tiled=True)
+    grad_context = (
+        dot(grad_attn, out_mat_t, ((1,), (0,))).astype(bf16).reshape(group_len, heads_local, HEAD)
+    )
+    grad_value_rows = (
+        jnp.einsum("hqk,qhd->khd", probs_low, grad_context, preferred_element_type=f32)
+        .reshape(group_len, -1)
+        .astype(bf16)
+    )
+    grad_probs = jnp.einsum("qhd,khd->hqk", grad_context, value_heads, preferred_element_type=f32)
+    grad_scores = (
+        attn_probs * (grad_probs - jnp.sum(attn_probs * grad_probs, axis=-1, keepdims=True))
+    ).astype(bf16)
+    grad_query_rot = rounded(
+        jnp.einsum("hqk,khd->qhd", grad_scores, key_rot, preferred_element_type=f32) * score_scale
+    )
+    grad_key_rot = rounded(
+        jnp.einsum("hqk,qhd->khd", grad_scores, query_rot, preferred_element_type=f32) * score_scale
+    )
+
+    def unrotate(grad_heads):
+        return (
+            grad_heads * cosine_table[:, None, :] + rotate_back(grad_heads * sine_table[:, None, :])
+        ).reshape(group_len, -1)
+
+    grad_query_norm = unrotate(grad_query_rot)
+    grad_key_norm = unrotate(grad_key_rot)
+    sums = jnp.stack(
+        [
+            jnp.sum(grad_query_norm * query_gain_flat * query_unit, axis=1),
+            jnp.sum(grad_key_norm * key_gain_flat * key_unit, axis=1),
+        ]
+    )
+    sums = (sums + swap_tp(sums)) / model_width
+    grad_query_raw = (
+        query_scale * (query_gain_flat * grad_query_norm - query_unit * sums[0][:, None])
+    ).astype(bf16)
+    grad_key_raw = (
+        key_scale * (key_gain_flat * grad_key_norm - key_unit * sums[1][:, None])
+    ).astype(bf16)
+    grad_gain_query = jnp.sum(grad_query_norm * query_unit, axis=0)
+    grad_gain_key = jnp.sum(grad_key_norm * key_unit, axis=0)
+    grad_qkv_raw = jnp.concatenate([grad_query_raw, grad_key_raw, grad_value_rows], axis=1)
+    grad_qkv = dot(normed_one, grad_qkv_raw, ((0,), (0,))).astype(bf16)
+    grad_qkv = lax.psum_scatter(grad_qkv, "fsdp", scatter_dimension=0, tiled=True)
+    grad_normed_part = dot(grad_qkv_raw, qkv_mat, ((1,), (1,))).astype(bf16)
+    grad_normed_one = own_sum(grad_normed_part)
+    scale_own = rms_scale(tokens_own)
+    normal_own = tokens_own * scale_own
+    grad_gain_attn = jnp.sum(grad_normed_one * normal_own, axis=0)
+    grad_unit_one = grad_normed_one * attn_gain
+    grad_tokens = grad_hidden + scale_own * (
+        grad_unit_one - normal_own * jnp.mean(grad_unit_one * normal_own, axis=1, keepdims=True)
+    )
+    block_out = hidden + own_sum(moe_group)
+
+    row_part = jnp.concatenate(
+        [
+            grad_router.reshape(fsdp_count, -1),
+            grad_gain_moe.reshape(fsdp_count, -1),
+            grad_gain_attn.reshape(fsdp_count, -1),
+        ],
+        axis=1,
+    )
+    row_part = row_part + swap_tp(row_part)
+
+    def by_owner(gain_grad):
+        pieces = gain_grad.reshape(heads_local, fsdp_count, gain_cols)
+        return jnp.transpose(pieces, (1, 0, 2)).reshape(fsdp_count, -1)
+
+    parcel = jnp.concatenate([row_part, by_owner(grad_gain_query), by_owner(grad_gain_key)], axis=1)
+    parcel = lax.all_to_all(parcel, "fsdp", split_axis=0, concat_axis=0, tiled=True)
+    parcel = jnp.sum(parcel, axis=0)
+    edges = [shard_rows * expert_count, shard_rows, shard_rows, gain_query.size, gain_key.size]
+    pieces, start = [], 0
+    for size in edges:
+        pieces.append(parcel[start : start + size])
+        start += size
+    grad_qkv = grad_qkv.astype(f32)
+    return (
+        block_out,
+        grad_tokens,
+        grad_qkv[:, :half_width],
+        grad_qkv[:, half_width : 2 * half_width],
+        grad_qkv[:, 2 * half_width :],
+        grad_output.astype(f32).T,
+        pieces[3].reshape(gain_query.shape),
+        pieces[4].reshape(gain_key.shape),
+        pieces[2],
+        pieces[1],
+        pieces[0].reshape(w_router.shape),
+        grad_gate[None],
+        grad_up[None],
+        grad_down[None],
+    )
+
+
+def body(*args):
+    topk_count = args[14].shape[1]
+    expert_count, local_experts = args[10].shape[1], args[11].shape[0]
+    if local_experts == 1 and lax.axis_size("tp") == 2 and expert_count <= 2 * topk_count:
+        return dense_body(*args)
+    return sparse_body(*args)
+
+
 def solution(mesh):
     in_specs = (
         P(("fsdp", "tp"), None),

time: 2090 us -> 1080 us (0.52)
  blocking collectives: 873 us -> 19.6 us
  local copies, waits for them, and re-layouts: 211 us -> 33.2 us
  matrix products: 136 us -> 204 us
  waiting for transfers between devices: 780 us -> 736 us
    all_to_all x3 -> x0, blocking collectives: 702 us -> none  [the longest x2 480 us: send_slots(): lax.all_to_all(block, 'fsdp', split_axis=0, concat_axis=0, tiled=True)]
    gather x18 -> x0, local copies, waits for them, and re-layouts: 156 us -> none  [the longest x8 68.5 us: body(): returned[slot_dest[:, column]].astype(jnp.float32)]
    all_to_all x1 -> x2, waiting for transfers between devices: 142 us -> 8.33 us  [the longest x1 4.83 us: dense_body(): lax.all_to_all(token_dots, 'fsdp', split_axis=0, concat_axis=0, tiled=True)]
    all_gather x6 -> x4, waiting for transfers between devices: 154 us -> 268 us  [the longest x1 92.2 us: dense_body(): rows_all = lax.all_gather(normed_two, both, axis=0, tiled=True)]
    psum x3 -> x0, waiting for transfers between devices: 80.9 us -> none  [the longest x1 56.9 us: body(): lax.psum((grad_normed_part, jnp.stack(gate_terms, axis=1)), 'tp')]
    all_gather x5 -> x1, blocking collectives: 96.4 us -> 19.6 us  [dense_body(): ids_all = lax.all_gather(expert_ids, 'fsdp', axis=0, tiled=True)]
    dot_general x31 -> x29, matrix products: 136 us -> 200 us  [the longest x20 137 us: dot(): lax.dot_general(left, right, (dims, ((), ())), preferred_element_type=f32)]
    unnamed x1 -> x0, blocking collectives: 60 us -> none
  transfers between devices with their start and end apart: 16 -> 20, of which waited for: 12 -> 15; matrix products, arithmetic and copies ran while one was open for 6% -> 17% of each run, Pallas kernels for 0% -> 0%
where the time goes in v1:
time: 1080 us; the launch traced here: 1070 us
  waiting for transfers between devices  736 us (68%)
  matrix products  204 us (19%)
  other arithmetic  43.3 us (4%)
  local copies, waits for them, and re-layouts  33.2 us (3%)
  starting transfers between devices  22.2 us (2%)
  blocking collectives  19.6 us (2%)
  between operations  15.4 us (1%)
    reduce_scatter x1, waiting for transfers between devices, dense_body(): lax.psum_scatter(grad_rows.reshape(-1, model_width), 'fsdp', scatter_dime...  148 us
    dot_general x20, matrix products, dot(): lax.dot_general(left, right, (dims, ((), ())), preferred_element_type=f32)  137 us
    reduce_scatter x1, waiting for transfers between devices, dense_body(): lax.psum_scatter(grad_qkv, 'fsdp', scatter_dimension=0, tiled=True)  136 us
    all_gather x1, waiting for transfers between devices, dense_body(): rows_all = lax.all_gather(normed_two, both, axis=0, tiled=True)  92.2 us
    all_gather x1, waiting for transfers between devices, dense_body(): packed_all = lax.all_gather(packed, 'fsdp', axis=0, tiled=True)  88.2 us
    reduce_scatter x1, waiting for transfers between devices, dense_body(): lax.psum_scatter(moe_out, 'fsdp', scatter_dimension=0, tiled=True)  74.6 us
    all_gather x1, waiting for transfers between devices, dense_body(): cotangent_all = lax.all_gather(cotangent, both, axis=0, tiled=True)  65.5 us
    ppermute x10, waiting for transfers between devices, swap_tp(): return lax.ppermute(values, 'tp', [(0, 1), (1, 0)])  58.3 us
  transfers between devices with their start and end apart: 20, of which 15 were waited for; matrix products, arithmetic and copies ran while one was open for 17% of the time, Pallas kernels for 0%

profile of v1, /device:TPU:0, one launch (start us, length us, event | category | flops | bytes accessed | tf_op | source)
XLA Modules:
  0.0 1073.7 jit_solution(8885633320245445944)
XLA Ops:
  10.5 2.1 fusion.61
  13.4 3.0 collective-permute-start
  17.2 11.5 %collective-permute-done = bf16[128,2048]{1,0:T(8,128)(2,1)} collective-permute-done((bf16[128,2048]{1,0:T(8,128)(2,1)}, bf16[128,2048]{1,0:T(8,128)(2,1)}, u32[]{:S(2)}, u32[]{:S(2)}) %collective-permute-start) | collective-permute-done | bytes 524320 | tf_op jit(solution)/shard_map/ppermute | solution.py:397
  30.9 88.2 %all-gather.5.cloned.1.call-done = bf16[2048,3200]{1,0:T(8,128)(2,1)} async-done(((bf16[128,3200]{1,0:T(8,128)(2,1)}), bf16[2048,3200]{1,0:T(8,128)(2,1)}) %all-gather.5.cloned.1.call-update) | async-done | bytes 13107216 | tf_op jit(solution)/shard_map/all_gather | solution.py:462
  119.1 2.0 convert_reduce_fusion
  121.2 6.6 fusion.3
  127.9 1.7 copy-done.3
  131.3 2.0 slice_reduce_fusion
  134.0 3.1 fusion.63
  137.1 1.6 copy.162
  138.6 2.5 copy.161
  144.1 3.5 fusion.112
  147.6 2.4 convolution_convert_fusion.6
  150.0 22.3 %all-gather.7.cloned.1.call-done = bf16[2048,1024]{0,1:T(8,128)(2,1)} async-done(((bf16[128,1024]{0,1:T(8,128)(2,1)}), bf16[2048,1024]{0,1:T(8,128)(2,1)}) %all-gather.7.cloned.1.call-update) | async-done | bytes 4194320 | tf_op jit(solution)/shard_map/all_gather | solution.py:475
  172.2 3.5 fusion.115
  177.4 12.6 %collective-permute-done.2 = bf16[128,2048]{1,0:T(8,128)(2,1)S(1)} collective-permute-done((bf16[128,2048]{1,0:T(8,128)(2,1)S(1)}, bf16[128,2048]{1,0:T(8,128)(2,1)S(1)}, u32[]{:S(2)}, u32[]{:S(2)}) %collective-permute-start.2) | collective-permute-done | bytes 524320 | tf_op jit(solution)/shard_map/ppermute | solution.py:397
  193.5 19.6 %all_gather.17 = s32[4096,8]{0,1:T(8,128)S(1)} all-gather(s32[256,8]{0,1:T(8,128)S(1)} %copy-done.46), channel_id=1, replica_groups=mesh['fsdp'=16,'tp'=2] {'fsdp'}, dimensions={0}, use_global_device_ids=true | all-gather | bytes 139264 | tf_op jit(solution)/shard_map/all_gather | solution.py:476
  213.6 92.2 %all-gather.9.cloned.1.call-done = bf16[4096,2048]{1,0:T(8,128)(2,1)} async-done(((bf16[128,2048]{1,0:T(8,128)(2,1)}), bf16[4096,2048]{1,0:T(8,128)(2,1)}) %all-gather.9.cloned.1.call-update) | async-done | bytes 16777232 | tf_op jit(solution)/shard_map/all_gather | solution.py:523
  305.8 10.3 fusion.113
  316.3 12.4 %convolution_convert_fusion.3 = bf16[16,152,2048]{2,1,0:T(8,128)(2,1)} fusion(bf16[16,256,2048]{2,1,0:T(8,128)(2,1)} %bitcast.132, s32[16,256]{1,0:T(8,128)S(1)} %convolution_convert_fusion.8, pred[16,256]{1,0:T(8,128)(4,1)S(1)} %reshape.472), kind=kOutput, calls=%fused_computation.12 | convolution fusion | flops 2556362752 | bytes 26759168 | tf_op jit(solution)/shard_map/gct,gtd->gcd/dot_general | solution.py:550
  328.7 9.8 fusion.25
  338.5 7.8 multiply_convert_fusion.4
  347.8 7.9 convolution_convert_fusion.1
  355.7 65.5 %all-gather.11.cloned.1.call-done = bf16[4096,2048]{1,0:T(8,128)(2,1)} async-done(((bf16[128,2048]{1,0:T(8,128)(2,1)}), bf16[4096,2048]{1,0:T(8,128)(2,1)}) %all-gather.11.cloned.1.call-update) | async-done | bytes 16777232 | tf_op jit(solution)/shard_map/all_gather | solution.py:524
  421.2 16.2 %multiply_reduce_fusion = (f32[16,152]{1,0:T(8,128)S(1)}, f32[16,152,2048]{2,1,0:T(8,128)}) fusion(bf16[16,152,2048]{2,1,0:T(8,128)(2,1)} %bitcast.135, bf16[16,256,2048]{2,1,0:T(8,128)(2,1)} %bitcast.137, s32[16,256]{1,0:T(8,128)S(1)} %convolution_convert_fusion.8, pred[16,256]{1,0:T(8,128)(4,1)S(1)} %reshape.472), kind=kOutput, calls=%fused_computation.2 | convolution fusion | flops 2566321664 | bytes 46691840 | tf_op jit(solution)/shard_map/gct,gtd->gcd/dot_general | solution.py:550
  437.4 1.6 select_reduce_fusion
  439.0 7.7 multiply_convert_fusion.1
  446.7 14.0 %multiply_convert_fusion.2 = (bf16[2432,512]{1,0:T(8,128)(2,1)S(1)}, bf16[2432,512]{1,0:T(8,128)(2,1)S(1)}) fusion(f32[2432,512]{1,0:T(8,128)} %copy-done.67, f32[2432,512]{1,0:T(8,128)} %get-tuple-element.136, bf16[2432,2048]{1,0:T(8,128)(2,1)S(1)} %bitcast.145, bf16[1,512,2048]{2,1,0:T(8,128)(2,1)S(1)} %copy-done), kind=kOutput, calls=%fused_computation.13 | convolution fusion | flops 5116461056 | bytes 27000832 | tf_op jit(solution)/shard_map/dot_general | solution.py:444
  460.8 9.7 fusion.23
  470.5 12.0 %add_convert_fusion = bf16[2432,2048]{1,0:T(8,128)(2,1)} fusion(f32[2432,2048]{1,0:T(8,128)} %fusion.23, bf16[2432,512]{1,0:T(8,128)(2,1)S(1)} %get-tuple-element.93, bf16[1,2048,512]{2,1,0:T(8,128)(2,1)S(1)} %copy-done.61), kind=kOutput, calls=%fused_computation.3 | convolution fusion | flops 5110235136 | bytes 34471936 | tf_op jit(solution)/shard_map/dot_general | solution.py:444
  482.5 12.0 %convolution_convert_fusion = bf16[16,256,2048]{2,1,0:T(8,128)(2,1)} fusion(bf16[16,152,2048]{2,1,0:T(8,128)(2,1)} %bitcast.144, s32[16,256]{1,0:T(8,128)S(1)} %convolution_convert_fusion.8, pred[16,256]{1,0:T(8,128)(4,1)S(1)} %reshape.472), kind=kOutput, calls=%fused_computation.5 | convolution fusion | flops 2559770624 | bytes 26759168 | tf_op jit(solution)/shard_map/gct,gcd->gtd/dot_general | solution.py:553
  494.5 15.8 %multiply_convert_fusion = bf16[16,256,2048]{2,1,0:T(8,128)(2,1)} fusion(f32[16,256]{1,0:T(8,128)S(1)} %mul.388, bf16[16,152,2048]{2,1,0:T(8,128)(2,1)} %bitcast.136, s32[16,256]{1,0:T(8,128)S(1)} %convolution_convert_fusion.8, pred[16,256]{1,0:T(8,128)(4,1)S(1)} %reshape.472), kind=kOutput, calls=%fused_computation.1 | convolution fusion | flops 2568159232 | bytes 26775552 | tf_op jit(solution)/shard_map/gct,gcd->gtd/dot_general | solution.py:553
  511.7 3.6 all-to-all-start
  515.3 1.6 fusion.114
  516.9 4.8 all-to-all-done
  522.5 147.7 %reduce-scatter.7.cloned.1.call-done = bf16[256,2048]{1,0:T(8,128)(2,1)} async-done(((bf16[4096,2048]{1,0:T(8,128)(2,1)}), bf16[256,2048]{1,0:T(8,128)(2,1)}) %reduce-scatter.7.cloned.1.call-update) | async-done | bytes 1048592 | tf_op jit(solution)/shard_map/reduce_scatter | solution.py:584
  671.5 1.5 collective-permute-start.4
  673.1 11.8 %collective-permute-done.4 = bf16[128,2048]{1,0:T(8,128)(2,1)S(1)} collective-permute-done((bf16[128,2048]{1,0:T(8,128)(2,1)S(1)}, bf16[128,2048]{1,0:T(8,128)(2,1)S(1)}, u32[]{:S(2)}, u32[]{:S(2)}) %collective-permute-start.4) | collective-permute-done | bytes 524320 | tf_op jit(solution)/shard_map/ppermute | solution.py:397
  684.9 2.3 multiply_reduce_fusion.4
  689.1 11.1 %collective-permute-done.6 = bf16[128,2048]{1,0:T(8,128)(2,1)S(1)} collective-permute-done((bf16[128,2048]{1,0:T(8,128)(2,1)S(1)}, bf16[128,2048]{1,0:T(8,128)(2,1)S(1)}, u32[]{:S(2)}, u32[]{:S(2)}) %collective-permute-start.6) | collective-permute-done | bytes 524320 | tf_op jit(solution)/shard_map/ppermute | solution.py:397
  700.3 3.3 convolution_convert_fusion.4
  703.7 3.5 convolution_convert_fusion.7
  707.4 2.6 multiply_reduce_fusion.1
  713.1 1.6 fusion.45
  714.7 1.6 copy.158
  716.3 1.6 copy.159
  717.9 2.3 multiply_reduce_fusion.2
  723.0 2.1 copy.160
  725.1 2.1 multiply_convert_fusion.7
  728.2 7.4 convolution_convert_fusion.2
  736.2 11.5 %convolution_bitcast_fusion = f32[1,512,2048]{2,1,0:T(8,128)} fusion(bf16[2432,512]{1,0:T(8,128)(2,1)} %copy-done.62, bf16[2432,2048]{1,0:T(8,128)(2,1)} %bitcast.146), kind=kOutput, calls=%fused_computation.19 | convolution fusion | flops 5100273664 | bytes 16646144 | tf_op jit(solution)/shard_map/dot_general | solution.py:444
  747.8 10.0 convolution_bitcast_fusion.1
  757.9 7.3 convolution_bitcast_fusion.2
  765.2 8.2 fusion.5
  776.0 74.6 %reduce-scatter.5.cloned.1.call-done = bf16[256,2048]{1,0:T(8,128)(2,1)} async-done(((bf16[4096,2048]{1,0:T(8,128)(2,1)}), bf16[256,2048]{1,0:T(8,128)(2,1)}) %reduce-scatter.5.cloned.1.call-update) | async-done | bytes 1048592 | tf_op jit(solution)/shard_map/reduce_scatter | solution.py:612
  851.9 1.5 collective-permute-start.3
  853.9 2.7 fusion.51
  857.2 11.3 %collective-permute-done.9 = f32[16,2304]{1,0:T(8,128)S(1)} collective-permute-done((f32[16,2304]{1,0:T(8,128)S(1)}, f32[16,2304]{1,0:T(8,128)S(1)}, u32[]{:S(2)}, u32[]{:S(2)}) %collective-permute-start.9) | collective-permute-done | bytes 147488 | tf_op jit(solution)/shard_map/ppermute | solution.py:397
  869.4 4.3 all-to-all-start.1
  873.7 4.8 fusion.50
  878.5 3.5 all-to-all-done.1
  884.8 41.6 %reduce-scatter.11.cloned.1.call-done = bf16[128,1024]{1,0:T(8,128)(2,1)} async-done(((bf16[2048,1024]{1,0:T(8,128)(2,1)}), bf16[128,1024]{1,0:T(8,128)(2,1)}) %reduce-scatter.11.cloned.1.call-update) | async-done | bytes 262160 | tf_op jit(solution)/shard_map/reduce_scatter | solution.py:611
  928.4 136.0 %reduce-scatter.9.cloned.1.call-done = bf16[128,3072]{1,0:T(8,128)(2,1)} async-done(((bf16[2048,3072]{1,0:T(8,128)(2,1)}), bf16[128,3072]{1,0:T(8,128)(2,1)}) %reduce-scatter.9.cloned.1.call-update) | async-done | bytes 786448 | tf_op jit(solution)/shard_map/reduce_scatter | solution.py:656
  1064.4 2.3 fusion.108
  (261 shorter events, 43.4 us)
Async XLA Ops:
  7.2 340.6 %copy-start = (bf16[1,512,2048]{2,1,0:T(8,128)(2,1)S(1)}, bf16[1,512,2048]{2,1,0:T(8,128)(2,1)}, u32[]{:S(2)}) copy-start(bf16[1,512,2048]{2,1,0:T(8,128)(2,1)} %param.28) | copy-start | bytes 6291460
  7.2 21.5 %copy-start.8 = (bf16[128,2048]{1,0:T(8,128)(2,1)S(1)}, bf16[128,2048]{1,0:T(8,128)(2,1)}, u32[]{:S(2)}) copy-start(bf16[128,2048]{1,0:T(8,128)(2,1)} %param.15) | copy-start | bytes 1572868
  7.2 111.9 %all-gather.5.cloned.1.call-start = ((), (), s32[]{:S(2)}) async-start(), calls=%async_computation.6 | async-start | bytes 13926400 | tf_op jit(solution)/shard_map/all_gather | solution.py:462
  12.6 159.6 %all-gather.7.cloned.1.call-start = ((), (), s32[]{:S(2)}) async-start(), calls=%async_computation.7 | async-start | bytes 4456448 | tf_op jit(solution)/shard_map/all_gather | solution.py:475
  13.3 292.4 %all-gather.9.cloned.1.call-start = ((), (), s32[]{:S(2)}) async-start(), calls=%async_computation.8 | async-start | bytes 17301504 | tf_op jit(solution)/shard_map/all_gather | solution.py:523
  13.4 15.3 %collective-permute-start = (bf16[128,2048]{1,0:T(8,128)(2,1)}, bf16[128,2048]{1,0:T(8,128)(2,1)}, u32[]{:S(2)}, u32[]{:S(2)}) collective-permute-start(bf16[128,2048]{1,0:T(8,128)(2,1)} %param.15), channel_id=1, source_target_pairs={{0,1},{1,0},{2,3},{3,2},{4,5},{5,4},{6,7},{7,6},{8,9},{9,8},{10,11... | collective-permute-start | bytes 1572872 | tf_op jit(solution)/shard_map/ppermute | solution.py:397
  17.0 125.6 %copy-start.24 = (f32[256,128]{0,1:T(8,128)}, f32[256,128]{0,1:T(8,128)S(1)}, u32[]{:S(2)}) copy-start(f32[256,128]{0,1:T(8,128)S(1)} %get-tuple-element.124) | copy-start | bytes 393220
  17.0 125.6 %copy-start.26 = (f32[256,128]{0,1:T(8,128)}, f32[256,128]{0,1:T(8,128)S(1)}, u32[]{:S(2)}) copy-start(f32[256,128]{0,1:T(8,128)S(1)} %get-tuple-element.123) | copy-start | bytes 393220
  29.8 98.0 %copy-start.16 = (bf16[128,2048]{1,0:T(8,128)(2,1)}, bf16[128,2048]{1,0:T(8,128)(2,1)S(1)}, u32[]{:S(2)}) copy-start(bf16[128,2048]{1,0:T(8,128)(2,1)S(1)} %get-tuple-element.111) | copy-start | bytes 1572868
  30.9 97.0 %copy-start.56 = (f32[256]{0:T(256)}, f32[256]{0:T(256)S(1)}, u32[]{:S(2)}) copy-start(f32[256]{0:T(256)S(1)} %add_rsqrt_fusion) | copy-start | bytes 3076
  121.2 6.7 copy-start.40
  121.2 69.7 %copy-start.38 = (f32[2048]{0:T(1024)}, f32[2048]{0:T(1024)S(1)}, u32[]{:S(2)}) copy-start(f32[2048]{0:T(1024)S(1)} %get-tuple-element.70) | copy-start | bytes 24580
  129.7 4.1 collective-permute-start.1
  133.6 3.5 copy-start.42
  149.9 25.8 %copy-start.28 = (bf16[8,128,256]{2,1,0:T(8,128)(2,1)}, bf16[8,128,256]{2,1,0:T(8,128)(2,1)S(1)}, u32[]{:S(2)}) copy-start(bf16[8,128,256]{2,1,0:T(8,128)(2,1)S(1)} %convolution_convert_fusion.6) | copy-start | bytes 1572868
  172.2 17.8 %copy-start.9 = (bf16[128,2048]{1,0:T(8,128)(2,1)S(1)}, bf16[128,2048]{1,0:T(8,128)(2,1)}, u32[]{:S(2)}) copy-start(bf16[128,2048]{1,0:T(8,128)(2,1)} %param.15) | copy-start | bytes 1572868
  175.8 17.6 %copy-start.46 = (s32[256,8]{0,1:T(8,128)S(1)}, s32[256,8]{0,1:T(8,128)}, u32[]{:S(2)}) copy-start(s32[256,8]{0,1:T(8,128)} %param.29) | copy-start | bytes 24580
  175.8 14.1 %collective-permute-start.2 = (bf16[128,2048]{1,0:T(8,128)(2,1)S(1)}, bf16[128,2048]{1,0:T(8,128)(2,1)S(1)}, u32[]{:S(2)}, u32[]{:S(2)}) collective-permute-start(bf16[128,2048]{1,0:T(8,128)(2,1)S(1)} %select_convert_fusion), channel_id=1, source_target_pairs={{0,1},{1,0},{2,3},{3,2},{4,5},{5,4},{6,7},{7,6},{8,9},{9,8},{10,11... | collective-permute-start | bytes 1572872 | tf_op jit(solution)/shard_map/ppermute | solution.py:397
  190.9 22.7 %copy-start.54 = (f32[128]{0:T(128)}, f32[128]{0:T(128)S(1)}, u32[]{:S(2)}) copy-start(f32[128]{0:T(128)S(1)} %add_rsqrt_fusion.2) | copy-start | bytes 1540
  192.8 228.4 %all-gather.11.cloned.1.call-start = ((), (), s32[]{:S(2)}) async-start(), calls=%async_computation.10 | async-start | bytes 17301504 | tf_op jit(solution)/shard_map/all_gather | solution.py:524
  193.4 476.8 %reduce-scatter.7.cloned.1.call-start = ((), (), s32[]{:S(2)}) async-start(), calls=%async_computation.11 | async-start | bytes 17825792 | tf_op jit(solution)/shard_map/reduce_scatter | solution.py:584
  328.7 9.8 copy-start.2
  328.7 9.8 copy-start.60
  338.5 7.8 copy-start.67
  446.7 14.0 %copy-start.6 = (bf16[16,152,2048]{2,1,0:T(8,128)(2,1)}, bf16[16,152,2048]{2,1,0:T(8,128)(2,1)S(1)}, u32[]{:S(2)}) copy-start(bf16[16,152,2048]{2,1,0:T(8,128)(2,1)S(1)} %multiply_convert_fusion.1) | copy-start | bytes 29884420
  446.7 14.0 %copy-start.59 = (bf16[1,2048,512]{2,1,0:T(8,128)(2,1)S(1)}, bf16[1,2048,512]{2,1,0:T(8,128)(2,1)}, u32[]{:S(2)}) copy-start(bf16[1,2048,512]{2,1,0:T(8,128)(2,1)} %param.26) | copy-start | bytes 6291460
  460.7 9.8 copy-start.63
  460.7 9.8 copy-start.65
  460.8 9.8 copy-start.61
  494.5 356.2 %reduce-scatter.5.cloned.1.call-start = ((), (), s32[]{:S(2)}) async-start(), calls=%async_computation.9 | async-start | bytes 17825792 | tf_op jit(solution)/shard_map/reduce_scatter | solution.py:612
  510.3 5.0 copy-start.11
  510.3 174.6 %copy-start.5 = (f32[128,2048]{1,0:T(8,128)S(1)}, f32[128,2048]{1,0:T(8,128)}, u32[]{:S(2)}) copy-start(f32[128,2048]{1,0:T(8,128)} %copy-done.4) | copy-start | bytes 3145732
  510.3 174.6 %copy-start.39 = (f32[2048]{0:T(1024)S(1)}, f32[2048]{0:T(1024)}, u32[]{:S(2)}) copy-start(f32[2048]{0:T(1024)} %copy-done.38) | copy-start | bytes 24580
  510.3 174.6 %copy-start.55 = (f32[128]{0:T(128)S(1)}, f32[128]{0:T(128)}, u32[]{:S(2)}) copy-start(f32[128]{0:T(128)} %copy-done.54) | copy-start | bytes 1540
  511.7 10.1 all-to-all-start
  515.3 172.0 %copy-start.13 = (bf16[128,2048]{1,0:T(8,128)(2,1)S(1)}, bf16[128,2048]{1,0:T(8,128)(2,1)}, u32[]{:S(2)}) copy-start(bf16[128,2048]{1,0:T(8,128)(2,1)} %param.16) | copy-start | bytes 1572868
  515.3 411.1 %reduce-scatter.11.cloned.1.call-start = ((), (), s32[]{:S(2)}) async-start(), calls=%async_computation.13 | async-start | bytes 4456448 | tf_op jit(solution)/shard_map/reduce_scatter | solution.py:611
  521.8 151.2 %collective-permute-start.5 = (f32[128,16]{0,1:T(8,128)S(1)}, f32[128,16]{0,1:T(8,128)S(1)}, u32[]{:S(2)}, u32[]{:S(2)}) collective-permute-start(f32[128,16]{0,1:T(8,128)S(1)} %slice_select_fusion), channel_id=1, source_target_pairs={{0,1},{1,0},{2,3},{3,2},{4,5},{5,4},{6,7},{7,6},{8,9},{9,8},{10,11... | collective-permute-start | bytes 24584 | tf_op jit(solution)/shard_map/ppermute | solution.py:397
  671.5 13.4 %collective-permute-start.4 = (bf16[128,2048]{1,0:T(8,128)(2,1)S(1)}, bf16[128,2048]{1,0:T(8,128)(2,1)S(1)}, u32[]{:S(2)}, u32[]{:S(2)}) collective-permute-start(bf16[128,2048]{1,0:T(8,128)(2,1)S(1)} %broadcast_select_fusion.4), channel_id=1, source_target_pairs={{0,1},{1,0},{2,3},{3,2},{4,5},{5,4},{6,7},{7,6},{8,9},{9,8},{10,11... | collective-permute-start | bytes 1572872 | tf_op jit(solution)/shard_map/ppermute | solution.py:397
  687.2 16.4 %copy-start.14 = (f32[128,2048]{1,0:T(8,128)}, f32[128,2048]{1,0:T(8,128)S(1)}, u32[]{:S(2)}) copy-start(f32[128,2048]{1,0:T(8,128)S(1)} %get-tuple-element.143) | copy-start | bytes 3145732
  687.2 13.1 %copy-start.29 = (bf16[8,128,256]{2,1,0:T(8,128)(2,1)S(1)}, bf16[8,128,256]{2,1,0:T(8,128)(2,1)}, u32[]{:S(2)}) copy-start(bf16[8,128,256]{2,1,0:T(8,128)(2,1)} %copy-done.28) | copy-start | bytes 1572868
  687.6 12.6 %collective-permute-start.6 = (bf16[128,2048]{1,0:T(8,128)(2,1)S(1)}, bf16[128,2048]{1,0:T(8,128)(2,1)S(1)}, u32[]{:S(2)}, u32[]{:S(2)}) collective-permute-start(bf16[128,2048]{1,0:T(8,128)(2,1)S(1)} %fusion.105), channel_id=1, source_target_pairs={{0,1},{1,0},{2,3},{3,2},{4,5},{5,4},{6,7},{7,6},{8,9},{9,8},{10,11... | collective-permute-start | bytes 1572872 | tf_op jit(solution)/shard_map/ppermute | solution.py:397
  703.6 3.8 copy-start.53
  703.7 360.7 %reduce-scatter.9.cloned.1.call-start = ((), (), s32[]{:S(2)}) async-start(), calls=%async_computation.12 | async-start | bytes 13369344 | tf_op jit(solution)/shard_map/reduce_scatter | solution.py:656
  717.9 3.8 copy-start.21
  717.9 3.8 copy-start.35
  720.2 4.9 collective-permute-start.7
  723.0 5.2 copy-start.41
  723.0 5.2 copy-start.57
  736.2 11.5 %copy-start.66 = (bf16[2432,512]{1,0:T(8,128)(2,1)S(1)}, bf16[2432,512]{1,0:T(8,128)(2,1)}, u32[]{:S(2)}) copy-start(bf16[2432,512]{1,0:T(8,128)(2,1)} %copy-done.65) | copy-start | bytes 7471108
  736.2 21.6 %slice-start = ((s8[9961472]{0:T(1024)(128)(4,1)}), s8[4194304]{0:T(1024)(128)(4,1)S(1)}, s32[]{:S(2)}) async-start(s8[9961472]{0:T(1024)(128)(4,1)} %bitcast.141), calls=%async_computation.14 | async-start | bytes 8388608
  736.2 21.6 %slice-start.1 = ((s8[9961472]{0:T(1024)(128)(4,1)}), s8[4194304]{0:T(1024)(128)(4,1)S(1)}, s32[]{:S(2)}) async-start(s8[9961472]{0:T(1024)(128)(4,1)} %bitcast.141), calls=%async_computation.15 | async-start | bytes 8388608
  747.8 10.0 slice-start.2
  747.8 10.0 copy-start.64
  757.8 7.3 copy-start.31
  757.8 7.3 copy-start.33
  757.9 7.3 copy-start.37
  765.2 9.9 copy-start.12
  773.4 80.5 %copy-start.10 = (bf16[128,2048]{1,0:T(8,128)(2,1)S(1)}, bf16[128,2048]{1,0:T(8,128)(2,1)}, u32[]{:S(2)}) copy-start(bf16[128,2048]{1,0:T(8,128)(2,1)} %param.15) | copy-start | bytes 1572868
  774.6 79.4 %collective-permute-start.8 = (bf16[128,2048]{1,0:T(8,128)(2,1)}, bf16[128,2048]{1,0:T(8,128)(2,1)}, u32[]{:S(2)}, u32[]{:S(2)}) collective-permute-start(bf16[128,2048]{1,0:T(8,128)(2,1)} %broadcast_select_fusion), channel_id=1, source_target_pairs={{0,1},{1,0},{2,3},{3,2},{4,5},{5,4},{6,7},{7,6},{8,9},{9,8},{10,11... | collective-permute-start | bytes 1572872 | tf_op jit(solution)/shard_map/ppermute | solution.py:397
  851.9 21.8 %collective-permute-start.3 = (bf16[128,2048]{1,0:T(8,128)(2,1)S(1)}, bf16[128,2048]{1,0:T(8,128)(2,1)}, u32[]{:S(2)}, u32[]{:S(2)}) collective-permute-start(bf16[128,2048]{1,0:T(8,128)(2,1)S(1)} %broadcast_select_fusion.5), channel_id=1, source_target_pairs={{0,1},{1,0},{2,3},{3,2},{4,5},{5,4},{6,7},{7,6},{8,9},{9,8},{10,11... | collective-permute-start | bytes 1572872 | tf_op jit(solution)/shard_map/ppermute | solution.py:397
  856.6 11.9 %collective-permute-start.9 = (f32[16,2304]{1,0:T(8,128)S(1)}, f32[16,2304]{1,0:T(8,128)S(1)}, u32[]{:S(2)}, u32[]{:S(2)}) collective-permute-start(f32[16,2304]{1,0:T(8,128)S(1)} %pad_maximum_fusion.7), channel_id=1, source_target_pairs={{0,1},{1,0},{2,3},{3,2},{4,5},{5,4},{6,7},{7,6},{8,9},{9,8},{10,11... | collective-permute-start | bytes 442376 | tf_op jit(solution)/shard_map/ppermute | solution.py:397
  869.4 12.6 %all-to-all-start.1 = ((f32[16,1,2432]{2,1,0:T(1,128)}), f32[16,1,2432]{2,1,0:T(1,128)S(1)}, u32[]{:S(2)}, u32[]{:S(2)}) async-start(f32[16,1,2432]{2,1,0:T(1,128)} %copy.148), calls=%async_computation.5 | async-start | bytes 311296 | tf_op jit(solution)/shard_map/all_to_all | solution.py:683
  873.7 193.0 %copy-start.1 = (bf16[1,512,2048]{2,1,0:T(8,128)(2,1)S(1)}, bf16[1,512,2048]{2,1,0:T(8,128)(2,1)}, u32[]{:S(2)}) copy-start(bf16[1,512,2048]{2,1,0:T(8,128)(2,1)} %param.28) | copy-start | bytes 6291460
  (27 other events, 54.6 us)
Sparse Core Ops, SparseCore 0:
  12.7 106.3 all-gather.4
  121.3 50.8 all-gather.6
  192.9 112.7 all-gather.8
  308.6 112.5 all-gather.10
  494.6 175.5 reduce-scatter.6
  674.2 176.4 reduce-scatter.4
  854.5 71.8 reduce-scatter.10
  930.5 133.9 reduce-scatter.8

commit v2 on v1

--- a/solution.py
+++ b/solution.py
@@ -2,6 +2,7 @@
 import jax.numpy as jnp
 from jax import lax
 from jax.sharding import PartitionSpec as P
+
 
 HEAD = 128
 PROMPT = 128
@@ -409,6 +410,57 @@
     return jnp.where(part_index == 0, low, high), jnp.where(part_index == 0, high, low)
 
 
+def fsdp_swap(values, stride, fsdp_count):
+    return lax.ppermute(values, "fsdp", [(i, i ^ stride) for i in range(fsdp_count)])
+
+
+def line_shift(values, senders, step, fsdp_count):
+    planes = fsdp_count // 4
+    pairs = [(z * 4 + low, (z + step) * 4 + low) for z in senders for low in range(4)]
+    return lax.ppermute(values, "fsdp", [p for p in pairs if 0 <= p[1] < planes * 4])
+
+
+def line_gather(own, plane, fsdp_count):
+    planes = fsdp_count // 4
+    right, left, from_low, from_high = own, own, [], []
+    for step in range(1, planes):
+        right = line_shift(right, range(step - 1, planes - 1), 1, fsdp_count)
+        left = line_shift(left, range(1, planes - step + 1), -1, fsdp_count)
+        from_low.append(right)
+        from_high.append(left)
+    relative = [own]
+    for step in range(1, planes):
+        relative.append(jnp.where(plane >= step, from_low[step - 1], from_high[planes - step - 1]))
+    wheel = [relative[(planes - 1 - i) % planes] for i in range(2 * planes - 1)]
+    return lax.dynamic_slice_in_dim(jnp.stack(wheel), planes - 1 - plane, planes, 0)
+
+
+def line_scatter(parts, plane, fsdp_count):
+    planes = fsdp_count // 4
+    wide = jnp.float32
+
+    def part(index):
+        return lax.dynamic_index_in_dim(parts, jnp.clip(index, 0, planes - 1), 0, keepdims=False)
+
+    right, left = None, None
+    for step in range(1, planes):
+        send_right = part(plane + planes - step)
+        send_left = part(plane - planes + step)
+        if step > 1:
+            send_right = (send_right.astype(wide) + right.astype(wide)).astype(parts.dtype)
+            send_left = (send_left.astype(wide) + left.astype(wide)).astype(parts.dtype)
+        right = line_shift(send_right, range(0, min(step, planes - 1)), 1, fsdp_count)
+        left = line_shift(send_left, range(max(planes - step, 1), planes), -1, fsdp_count)
+    total = part(plane).astype(wide)
+    if planes > 1:
+        total = total + right.astype(wide) + left.astype(wide)
+    return total
+
+
+def ordered(own, other, index, axis):
+    return jnp.stack([jnp.where(index == 0, own, other), jnp.where(index == 0, other, own)], axis)
+
+
 def dense_body(
     tokens_in,
     cotangent,
@@ -446,6 +498,10 @@
     def column(flat):
         return jnp.pad(flat, (0, shard_rows - flat.shape[0]))[:, None]
 
+    expert_row = jnp.arange(expert_count, dtype=jnp.int32)
+    mask_group = jnp.any(expert_ids[:, :, None] == expert_row[None, None, :], axis=1)
+    mask_packed = mask_group.astype(bf16).reshape(shard_rows, -1)
+    mask_cols = mask_packed.shape[1]
     small = jnp.concatenate(
         [
             w_router,
@@ -453,13 +509,24 @@
             gain_moe[:, None],
             column(gain_query.reshape(-1)),
             column(gain_key.reshape(-1)),
+            mask_packed,
         ],
         axis=1,
     )
     small_cols = small.shape[1]
-    small = jnp.pad(small, ((0, 0), (0, 128 - small_cols)))
+    small = jnp.pad(small, ((0, 0), (0, -small_cols % 128)))
     packed = jnp.concatenate([w_query, w_key, w_value, small], axis=1)
     packed_all = lax.all_gather(packed, "fsdp", axis=0, tiled=True)
+    plane, row_y, core = expert_index // 4, expert_index // 2 % 2, expert_index % 2
+    planes = fsdp_count // 4
+    cot_line = line_gather(cotangent, plane, fsdp_count)
+    cot_line = ordered(cot_line, fsdp_swap(cot_line, 2, fsdp_count), row_y, 1)
+    packed_all, cot_line = lax.optimization_barrier((packed_all, cot_line))
+    cot_across = swap_tp(cot_line)
+    cot_core = ordered(cot_line, cot_across, part_index, 2)
+    cot_core = cot_core.reshape(2 * planes, group_len, model_width)
+    cot_partner = fsdp_swap(cot_core, 1, fsdp_count)
+
     qkv_mat = packed_all[:, : 3 * half_width]
     small_all = packed_all[:, 3 * half_width :]
     router_mat = small_all[:, :expert_count]
@@ -473,7 +540,7 @@
 
     query_gain_flat, key_gain_flat = head_gain(0), head_gain(1)
     out_mat_t = lax.all_gather(w_output.T, "fsdp", axis=0, tiled=True)
-    ids_all = lax.all_gather(expert_ids, "fsdp", axis=0, tiled=True)
+    mask_all = small_all[:, small_cols - mask_cols : small_cols].reshape(-1, expert_count) > 0
 
     residual_in = joined_rows(tokens_in, swap_tp(tokens_in), part_index).astype(f32)
     scale_one = rms_scale(residual_in)
@@ -521,11 +588,6 @@
 
     both = ("fsdp", "tp")
     rows_all = lax.all_gather(normed_two, both, axis=0, tiled=True)
-    cotangent_all = lax.all_gather(cotangent, both, axis=0, tiled=True)
-    expert_row = jnp.arange(expert_count, dtype=jnp.int32)
-
-    def chosen_mask(ids):
-        return jnp.any(ids[:, :, None] == expert_row[None, None, :], axis=1)
 
     def gates_of(rows, mask):
         logits = jnp.where(mask, dot(rows, router_mat, ((1,), (0,))), -jnp.inf)
@@ -533,10 +595,11 @@
         weights = jnp.where(mask, jnp.exp(logits - top), 0.0)
         return weights / jnp.sum(weights, axis=1, keepdims=True)
 
-    gates_all = gates_of(rows_all, chosen_mask(ids_all))
+    gates_all = gates_of(rows_all, mask_all)
     gate_here = jnp.sum(jnp.where(expert_row[None, :] == expert_index, gates_all, 0.0), axis=1)
     gate_here = gate_here.reshape(fsdp_count, group_len)
-    named = jnp.any(ids_all == expert_index, axis=1).reshape(fsdp_count, group_len)
+    named = jnp.any(mask_all & (expert_row[None, :] == expert_index), axis=1)
+    named = named.reshape(fsdp_count, group_len)
     row_index = jnp.arange(group_len, dtype=jnp.int32)
     earlier = (row_index[:, None] < row_index[None, :]).astype(bf16)
     place = dot(named.astype(bf16), earlier, ((1,), (0,))).astype(jnp.int32)
@@ -545,15 +608,21 @@
     select_low = select.astype(bf16)
     gate_slot = jnp.sum(jnp.where(select, gate_here[:, None, :], 0.0), axis=2)
 
-    def pick(rows):
-        grouped = rows.reshape(fsdp_count, group_len, model_width)
-        return jnp.einsum("gct,gtd->gcd", select_low, grouped, preferred_element_type=f32)
-
-    def spread(slots):
-        return jnp.einsum("gct,gcd->gtd", select_low, slots, preferred_element_type=f32)
+    def pick(chosen, rows):
+        return jnp.einsum("gct,gtd->gcd", chosen, rows, preferred_element_type=f32).astype(bf16)
+
+    def spread(chosen, slots):
+        return jnp.einsum("gct,gcd->gtd", chosen, slots, preferred_element_type=f32)
+
+    def of_core(values, index):
+        paired = values.reshape((2 * planes, 2) + values.shape[1:])
+        return lax.dynamic_index_in_dim(paired, index, 1, keepdims=False)
+
+    select_mine, select_partner = of_core(select_low, core), of_core(select_low, 1 - core)
 
     slot_count = fsdp_count * capacity
-    arrived = pick(rows_all).astype(bf16).reshape(slot_count, model_width)
+    arrived = pick(select_low, rows_all.reshape(fsdp_count, group_len, model_width))
+    arrived = arrived.reshape(slot_count, model_width)
     gate_mat, up_mat, down_mat = w_gate[0], w_up[0], w_down[0]
     gate_pre = dot(arrived, gate_mat, ((1,), (0,)))
     up_pre = dot(arrived, up_mat, ((1,), (0,)))
@@ -561,11 +630,13 @@
     activation = (gate_pre * gate_sig * up_pre).astype(bf16)
     partial_value = dot(activation, down_mat, ((1,), (0,))).astype(bf16)
     partial_value = partial_value.reshape(fsdp_count, capacity, model_width)
-    cotangent_slot = pick(cotangent_all)
+    cotangent_slot = ordered(
+        pick(select_mine, cot_core), pick(select_partner, cot_partner), core, 1
+    )
+    cotangent_slot = cotangent_slot.reshape(fsdp_count, capacity, model_width).astype(f32)
     slot_dots = jnp.sum(cotangent_slot * partial_value.astype(f32), axis=2)
     token_dots = jnp.sum(jnp.where(select, slot_dots[:, :, None], 0.0), axis=1)
-    moe_out = (spread(partial_value) * gate_here[:, :, None]).astype(bf16)
-    moe_out = moe_out.reshape(-1, model_width)
+
     dots_owned = lax.all_to_all(token_dots, "fsdp", split_axis=0, concat_axis=0, tiled=True)
     dots_own, dots_other = halves_of(dots_owned.T, part_index)
     grad_gates = dots_own + swap_tp(dots_other)
@@ -580,10 +651,35 @@
     grad_in = (
         dot(grad_gate_pre, gate_mat, ((1,), (1,))) + dot(grad_up_pre, up_mat, ((1,), (1,)))
     ).astype(bf16)
-    grad_rows = spread(grad_in.reshape(fsdp_count, capacity, model_width)).astype(bf16)
+    grad_rows = spread(select_low, grad_in.reshape(fsdp_count, capacity, model_width)).astype(bf16)
+    grad_rows, partial_value = lax.optimization_barrier((grad_rows, partial_value))
+
+    def weighted(index, chosen):
+        slots = of_core(partial_value, index)
+        return spread(chosen, slots) * of_core(gate_here, index)[:, :, None]
+
+    moe_away = weighted(1 - core, select_partner).astype(bf16)
+    moe_sum = (
+        weighted(core, select_mine) + fsdp_swap(moe_away, 1, fsdp_count).astype(f32)
+    ).astype(bf16)
+    moe_sum = moe_sum.reshape(2 * planes, 2, own_rows, model_width)
+
     grad_group = lax.psum_scatter(
         grad_rows.reshape(-1, model_width), "fsdp", scatter_dimension=0, tiled=True
     )
+    grad_group, moe_sum = lax.optimization_barrier((grad_group, moe_sum))
+
+    def keep_and_send(values, index, axis):
+        keep = lax.dynamic_index_in_dim(values, index, axis, keepdims=False)
+        return keep, lax.dynamic_index_in_dim(values, 1 - index, axis, keepdims=False)
+
+    moe_keep, moe_away = keep_and_send(moe_sum, part_index, 1)
+    moe_across = swap_tp(moe_away)
+    moe_sum = (moe_keep.astype(f32) + moe_across.astype(f32)).astype(bf16)
+    moe_sum = moe_sum.reshape(planes, 2, own_rows, model_width)
+    moe_keep, moe_away = keep_and_send(moe_sum, row_y, 1)
+    moe_sum = moe_keep.astype(f32) + fsdp_swap(moe_away, 2, fsdp_count).astype(f32)
+    moe_own = line_scatter(moe_sum.astype(bf16), plane, fsdp_count)
     grad_down = dot(activation, grad_slot, ((0,), (0,)))
     grad_gate = dot(arrived, grad_gate_pre, ((0,), (0,)))
     grad_up = dot(arrived, grad_up_pre, ((0,), (0,)))
@@ -592,8 +688,8 @@
         own, other = halves_of(group_rows, part_index)
         return own.astype(f32) + swap_tp(other).astype(f32)
 
-    own_ids, _ = halves_of(expert_ids, part_index)
-    gates_own = gates_of(normed_two, chosen_mask(own_ids))
+    own_mask, _ = halves_of(mask_group, part_index)
+    gates_own = gates_of(normed_two, own_mask)
     grad_logits = (
         gates_own * (grad_gates - jnp.sum(gates_own * grad_gates, axis=1, keepdims=True))
     ).astype(bf16)
@@ -609,10 +705,8 @@
 
     grad_output = dot(grad_attn, context_flat, ((0,), (0,)))
     grad_output = lax.psum_scatter(grad_output.astype(bf16), "fsdp", scatter_dimension=0, tiled=True)
-    moe_group = lax.psum_scatter(moe_out, "fsdp", scatter_dimension=0, tiled=True)
-    grad_context = (
-        dot(grad_attn, out_mat_t, ((1,), (0,))).astype(bf16).reshape(group_len, heads_local, HEAD)
-    )
+    grad_context = dot(grad_attn, out_mat_t, ((1,), (0,))).astype(bf16)
+    grad_context = grad_context.reshape(group_len, heads_local, HEAD)
     grad_value_rows = (
         jnp.einsum("hqk,qhd->khd", probs_low, grad_context, preferred_element_type=f32)
         .reshape(group_len, -1)
@@ -663,7 +757,7 @@
     grad_tokens = grad_hidden + scale_own * (
         grad_unit_one - normal_own * jnp.mean(grad_unit_one * normal_own, axis=1, keepdims=True)
     )
-    block_out = hidden + own_sum(moe_group)
+    block_out = hidden + moe_own
 
     row_part = jnp.concatenate(
         [
@@ -709,7 +803,8 @@
 def body(*args):
     topk_count = args[14].shape[1]
     expert_count, local_experts = args[10].shape[1], args[11].shape[0]
-    if local_experts == 1 and lax.axis_size("tp") == 2 and expert_count <= 2 * topk_count:
+    paired = lax.axis_size("tp") == 2 and lax.axis_size("fsdp") % 4 == 0
+    if local_experts == 1 and paired and expert_count <= 2 * topk_count:
         return dense_body(*args)
     return sparse_body(*args)
 

time: 1080 us -> 1070 us (level)
  waiting for transfers between devices: 736 us -> 603 us
  other arithmetic: 43.3 us -> 104 us
  local copies, waits for them, and re-layouts: 33.2 us -> 75.1 us
  starting transfers between devices: 22.2 us -> 55.7 us
  blocking collectives: 19.6 us -> 0 us
    ppermute x0 -> x16, waiting for transfers between devices: none -> 216 us  [the longest x12 130 us: line_shift(): lax.ppermute(values, 'fsdp', [p for p in pairs if 0 <= p[1] < planes * 4])]
    ppermute x10 -> x11, waiting for transfers between devices: 58.3 us -> 239 us  [swap_tp(): return lax.ppermute(values, 'tp', [(0, 1), (1, 0)])]
    reduce_scatter x1, waiting for transfers between devices: 136 us -> 0.01 us  [dense_body(): lax.psum_scatter(grad_qkv, 'fsdp', scatter_dimension=0, tiled=True)]
    all_gather x1, waiting for transfers between devices: 92.2 us -> 0.02 us  [dense_body(): rows_all = lax.all_gather(normed_two, both, axis=0, tiled=True)]
    all_gather x1, waiting for transfers between devices: 88.2 us -> 0.01 us  [dense_body(): packed_all = lax.all_gather(packed, 'fsdp', axis=0, tiled=True)]
    reduce_scatter x1 -> x0, waiting for transfers between devices: 74.6 us -> none  [dense_body(): lax.psum_scatter(moe_out, 'fsdp', scatter_dimension=0, tiled=True)]
    all_gather x1 -> x0, waiting for transfers between devices: 65.5 us -> none  [dense_body(): cotangent_all = lax.all_gather(cotangent, both, axis=0, tiled=True)]
    reduce_scatter x1, waiting for transfers between devices: 41.6 us -> 0.01 us  [dense_body(): lax.psum_scatter(grad_output.astype(bf16), 'fsdp', scatter_dimension=0, t...]
  transfers between devices with their start and end apart: 20 -> 35, of which waited for: 15 -> 18; matrix products, arithmetic and copies ran while one was open for 17% -> 23% of each run, Pallas kernels for 0% -> 0%
where the time goes in v2:
time: 1070 us; the launch traced here: 1060 us
  waiting for transfers between devices  603 us (56%)
  matrix products  210 us (20%)
  other arithmetic  104 us (10%)
  local copies, waits for them, and re-layouts  75.1 us (7%)
  starting transfers between devices  55.7 us (5%)
  between operations  15.8 us (1%)
    ppermute x11, waiting for transfers between devices, swap_tp(): return lax.ppermute(values, 'tp', [(0, 1), (1, 0)])  239 us
    dot_general x20, matrix products, dot(): lax.dot_general(left, right, (dims, ((), ())), preferred_element_type=f32)  142 us
    reduce_scatter x1, waiting for transfers between devices, dense_body(): lax.psum_scatter(grad_rows.reshape(-1, model_width), 'fsdp', scatter_dime...  132 us
    ppermute x12, waiting for transfers between devices, line_shift(): lax.ppermute(values, 'fsdp', [p for p in pairs if 0 <= p[1] < planes * 4])  130 us
    ppermute x4, waiting for transfers between devices, fsdp_swap(): lax.ppermute(values, 'fsdp', [(i, i ^ stride) for i in range(fsdp_count)])  85.7 us
    dot_general x3, matrix products, spread(): return jnp.einsum('gct,gcd->gtd', chosen, slots, preferred_element_type=f32)  31.6 us
    ppermute x12, starting transfers between devices, line_shift(): lax.ppermute(values, 'fsdp', [p for p in pairs if 0 <= p[1] < planes * 4])  28.1 us
    dot_general x3, matrix products, pick(): jnp.einsum('gct,gtd->gcd', chosen, rows, preferred_element_type=f32)  26.2 us
  transfers between devices with their start and end apart: 35, of which 18 were waited for; matrix products, arithmetic and copies ran while one was open for 23% of the time, Pallas kernels for 0%

profile of v2, /device:TPU:0, one launch (start us, length us, event | category | flops | bytes accessed | tf_op | source)
XLA Modules:
  0.0 1063.8 jit_solution(11643504392654146230)
XLA Ops:
  14.4 5.0 collective-permute-start.1
  20.7 15.6 %collective-permute-done.1 = bf16[128,2048]{1,0:T(8,128)(2,1)S(1)} collective-permute-done((bf16[128,2048]{1,0:T(8,128)(2,1)}, bf16[128,2048]{1,0:T(8,128)(2,1)S(1)}, u32[]{:S(2)}, u32[]{:S(2)}) %collective-permute-start.1) | collective-permute-done | bytes 524320 | tf_op jit(solution)/shard_map/ppermute | solution.py:420
  37.8 12.7 %collective-permute-done.4 = bf16[128,2048]{1,0:T(8,128)(2,1)} collective-permute-done((bf16[128,2048]{1,0:T(8,128)(2,1)}, bf16[128,2048]{1,0:T(8,128)(2,1)}, u32[]{:S(2)}, u32[]{:S(2)}) %collective-permute-start.4) | collective-permute-done | bytes 524320 | tf_op jit(solution)/shard_map/ppermute | solution.py:420
  53.4 19.2 %collective-permute-done.5 = bf16[128,2048]{1,0:T(8,128)(2,1)} collective-permute-done((bf16[128,2048]{1,0:T(8,128)(2,1)}, bf16[128,2048]{1,0:T(8,128)(2,1)}, u32[]{:S(2)}, u32[]{:S(2)}) %collective-permute-start.5) | collective-permute-done | bytes 524320 | tf_op jit(solution)/shard_map/ppermute | solution.py:420
  76.3 45.9 %collective-permute-done.6 = bf16[128,2048]{1,0:T(8,128)(2,1)S(1)} collective-permute-done((bf16[128,2048]{1,0:T(8,128)(2,1)}, bf16[128,2048]{1,0:T(8,128)(2,1)S(1)}, u32[]{:S(2)}, u32[]{:S(2)}) %collective-permute-start.6) | collective-permute-done | bytes 524320 | tf_op jit(solution)/shard_map/ppermute | solution.py:420
  127.5 4.7 collective-permute-start.7
  134.4 9.4 collective-permute-done
  145.7 39.3 %collective-permute-done.7 = bf16[4,128,2048]{2,1,0:T(8,128)(2,1)} collective-permute-done((bf16[4,128,2048]{2,1,0:T(8,128)(2,1)}, bf16[4,128,2048]{2,1,0:T(8,128)(2,1)}, u32[]{:S(2)}, u32[]{:S(2)}) %collective-permute-start.7) | collective-permute-done | bytes 2097184 | tf_op jit(solution)/shard_map/ppermute | solution.py:414
  185.0 2.5 select_bitcast_fusion.5
  191.9 6.5 fusion.5
  204.3 3.1 fusion.78
  209.0 2.5 copy.214
  214.4 3.4 fusion.131
  220.1 3.6 fusion.136
  225.0 12.4 %collective-permute-done.9 = bf16[128,2048]{1,0:T(8,128)(2,1)S(1)} collective-permute-done((bf16[128,2048]{1,0:T(8,128)(2,1)S(1)}, bf16[128,2048]{1,0:T(8,128)(2,1)S(1)}, u32[]{:S(2)}, u32[]{:S(2)}) %collective-permute-start.9) | collective-permute-done | bytes 524320 | tf_op jit(solution)/shard_map/ppermute | solution.py:398
  241.5 130.2 %collective-permute-done.10 = bf16[4,2,128,2048]{3,2,0,1:T(8,128)(2,1)S(1)} collective-permute-done((bf16[4,2,128,2048]{3,2,0,1:T(8,128)(2,1)}, bf16[4,2,128,2048]{3,2,0,1:T(8,128)(2,1)S(1)}, u32[]{:S(2)}, u32[]{:S(2)}) %collective-permute-start.10) | collective-permute-done | bytes 4194336 | tf_op jit(solution)/shard_map/ppermute | solution.py:398
  371.7 4.2 select_bitcast_fusion.3
  375.9 6.6 pad_maximum_fusion
  382.4 8.4 copy.177
  394.0 5.1 convolution_convert_fusion.5
  399.1 5.2 collective-permute-done.11
  404.3 8.7 select_bitcast_fusion.1
  413.0 11.9 %maximum_convert_fusion = f32[8,2,152,2048]{3,2,0,1:T(8,128)} fusion(bf16[8,1,152,2048]{3,2,0,1:T(8,128)(2,1)} %get-tuple-element.108, bf16[8,1,152,2048]{3,2,0,1:T(8,128)(2,1)} %get-tuple-element.107), kind=kLoop, calls=%fused_computation.16 | loop fusion | flops 9961472 | bytes 29884416 | tf_op jit(solution)/shard_map/convert_element_type | solution.py:636
  424.9 15.0 %copy.186 = f32[8,2,152,2048]{3,2,1,0:T(8,128)} copy(f32[8,2,152,2048]{3,2,0,1:T(8,128)} %maximum_convert_fusion) | data formatting | bytes 39845888 | tf_op jit(solution)/shard_map/convert_element_type | solution.py:636
  439.9 10.3 fusion.132
  450.5 12.4 %convolution_convert_fusion.3 = bf16[16,152,2048]{2,1,0:T(8,128)(2,1)} fusion(bf16[16,256,2048]{2,1,0:T(8,128)(2,1)} %bitcast.225, s32[16,256]{1,0:T(8,128)S(1)} %convolution_convert_fusion.10, pred[16,256]{1,0:T(8,128)(4,1)S(1)} %reshape.550), kind=kOutput, calls=%fused_computation.20 | convolution fusion | flops 2556362752 | bytes 26759168 | tf_op jit(solution)/shard_map/gct,gtd->gcd/dot_general | solution.py:612
  462.9 9.1 fusion.25
  472.0 7.8 multiply_convert_fusion.2
  479.8 12.9 %fusion.1 = (f32[2432]{0:T(1024)S(1)}, bf16[2432,2048]{1,0:T(8,128)(2,1)}) fusion(f32[8,2,152,2048]{3,2,1,0:T(8,128)} %copy.186, bf16[2432,512]{1,0:T(8,128)(2,1)S(1)} %get-tuple-element.159, bf16[1,512,2048]{2,1,0:T(8,128)(2,1)S(1)} %copy-done), kind=kOutput, calls=%fused_computation.3 | convolution fusion | flops 5120194048 | bytes 34481664 | tf_op jit(solution)/shard_map/dot_general | solution.py:496
  494.4 9.9 multiply_convert_fusion
  504.3 9.6 copy.181
  513.9 12.7 %multiply_convert_fusion.3 = (bf16[2432,512]{1,0:T(8,128)(2,1)S(1)}, bf16[2432,512]{1,0:T(8,128)(2,1)S(1)}) fusion(f32[2432,512]{1,0:T(8,128)} %copy-done.70, f32[2432,512]{1,0:T(8,128)} %get-tuple-element.160, bf16[2432,2048]{1,0:T(8,128)(2,1)} %bitcast.242, bf16[1,512,2048]{2,1,0:T(8,128)(2,1)S(1)} %copy-done), kind=kOutput, calls=%fused_computation.26 | convolution fusion | flops 5116461056 | bytes 27000832 | tf_op jit(solution)/shard_map/dot_general | solution.py:496
  526.7 9.8 fusion.23
  536.6 11.9 %add_convert_fusion = bf16[2432,2048]{1,0:T(8,128)(2,1)} fusion(f32[2432,2048]{1,0:T(8,128)} %fusion.23, bf16[2432,512]{1,0:T(8,128)(2,1)S(1)} %get-tuple-element.105, bf16[1,2048,512]{2,1,0:T(8,128)(2,1)S(1)} %copy-done.66), kind=kOutput, calls=%fused_computation.5 | convolution fusion | flops 5110235136 | bytes 34471936 | tf_op jit(solution)/shard_map/dot_general | solution.py:496
  548.5 12.0 %convolution_convert_fusion = bf16[16,256,2048]{2,1,0:T(8,128)(2,1)} fusion(bf16[16,152,2048]{2,1,0:T(8,128)(2,1)} %bitcast.239, s32[16,256]{1,0:T(8,128)S(1)} %convolution_convert_fusion.10, pred[16,256]{1,0:T(8,128)(4,1)S(1)} %reshape.550), kind=kOutput, calls=%fused_computation.9 | convolution fusion | flops 2559770624 | bytes 26759168 | tf_op jit(solution)/shard_map/gct,gcd->gtd/dot_general | solution.py:615
  560.6 7.5 multiply_convert_fusion.1
  568.8 4.0 all-to-all-start
  574.6 16.1 %all-to-all-done = f32[16,1,256]{2,1,0:T(1,128)S(1)} async-done(((f32[16,1,256]{2,1,0:T(1,128)}), f32[16,1,256]{2,1,0:T(1,128)S(1)}, u32[]{:S(2)}, u32[]{:S(2)}) %all-to-all-start) | async-done | bytes 16416 | tf_op jit(solution)/shard_map/all_to_all | solution.py:640
  592.3 12.0 %add_convert_fusion.1 = bf16[8,256,2048]{2,1,0:T(8,128)(2,1)} fusion(bf16[8,256,2048]{2,1,0:T(8,128)(2,1)} %collective-permute-done.12, f32[8,256]{1,0:T(8,128)S(1)} %bitcast.268, bf16[8,2,152,2048]{3,2,1,0:T(8,128)(2,1)} %bitcast.228, s32[]{:T(128)S(6)} %select_n.268, pred[8,2,152,256]{3,2,0,1:T(8,128)(4,1)} %copy-done.16), kind=kOutput, calls=%fused_computation.7 | convolution fusion | flops 1291845632 | bytes 22078464 | tf_op jit(solution)/shard_map/gct,gcd->gtd/dot_general | solution.py:615
  604.3 132.2 %reduce-scatter.4.cloned.1.call-done = bf16[256,2048]{1,0:T(8,128)(2,1)} async-done(((bf16[4096,2048]{1,0:T(8,128)(2,1)}), bf16[256,2048]{1,0:T(8,128)(2,1)}) %reduce-scatter.4.cloned.1.call-update) | async-done | bytes 1048592 | tf_op jit(solution)/shard_map/reduce_scatter | solution.py:667
  739.3 11.8 %collective-permute-done.21 = bf16[128,2048]{1,0:T(8,128)(2,1)S(1)} collective-permute-done((bf16[128,2048]{1,0:T(8,128)(2,1)S(1)}, bf16[128,2048]{1,0:T(8,128)(2,1)S(1)}, u32[]{:S(2)}, u32[]{:S(2)}) %collective-permute-start.21) | collective-permute-done | bytes 524320 | tf_op jit(solution)/shard_map/ppermute | solution.py:398
  755.0 11.0 %collective-permute-done.23 = bf16[128,2048]{1,0:T(8,128)(2,1)S(1)} collective-permute-done((bf16[128,2048]{1,0:T(8,128)(2,1)S(1)}, bf16[128,2048]{1,0:T(8,128)(2,1)S(1)}, u32[]{:S(2)}, u32[]{:S(2)}) %collective-permute-start.23) | collective-permute-done | bytes 524320 | tf_op jit(solution)/shard_map/ppermute | solution.py:398
  766.2 3.3 convolution_convert_fusion.6
  769.6 3.5 convolution_convert_fusion.9
  773.3 2.7 multiply_reduce_fusion
  783.8 2.4 multiply_reduce_fusion.1
  794.1 7.3 convolution_convert_fusion.2
  801.5 4.8 dynamic-slice_bitcast_fusion
  807.1 11.6 %convolution_bitcast_fusion.1 = f32[1,2048,512]{2,1,0:T(8,128)} fusion(bf16[2432,2048]{1,0:T(8,128)(2,1)} %bitcast.234, bf16[2432,512]{1,0:T(8,128)(2,1)} %copy-done.69), kind=kOutput, calls=%fused_computation.42 | convolution fusion | flops 5100273664 | bytes 16646144 | tf_op jit(solution)/shard_map/dot_general | solution.py:496
  818.7 13.9 %fusion.2 = bf16[2432,2048]{1,0:T(8,128)(2,1)} fusion(f32[8,2,152,2048]{3,2,1,0:T(8,128)} %copy.186, f32[2432]{0:T(1024)S(1)} %mul.472), kind=kLoop, calls=%fused_computation.4 | loop fusion | flops 9961472 | bytes 29894144 | tf_op jit(solution)/shard_map/convert_element_type | solution.py:644
  832.6 64.3 %collective-permute-done.13 = bf16[8,128,2048]{2,1,0:T(8,128)(2,1)} collective-permute-done((bf16[8,128,2048]{2,1,0:T(8,128)(2,1)}, bf16[8,128,2048]{2,1,0:T(8,128)(2,1)}, u32[]{:S(2)}, u32[]{:S(2)}) %collective-permute-start.13) | collective-permute-done | bytes 4194336 | tf_op jit(solution)/shard_map/ppermute | solution.py:398
  897.0 5.5 fusion.7
  906.0 7.3 convolution_bitcast_fusion.2
  914.7 8.6 fusion.13
  924.3 41.3 %collective-permute-done.14 = bf16[4,128,2048]{2,1,0:T(8,128)(2,1)} collective-permute-done((bf16[4,128,2048]{2,1,0:T(8,128)(2,1)}, bf16[4,128,2048]{2,1,0:T(8,128)(2,1)}, u32[]{:S(2)}, u32[]{:S(2)}) %collective-permute-start.14) | collective-permute-done | bytes 2097184 | tf_op jit(solution)/shard_map/ppermute | solution.py:414
  974.1 18.3 %collective-permute-done.15 = bf16[128,2048]{1,0:T(8,128)(2,1)S(1)} collective-permute-done((bf16[128,2048]{1,0:T(8,128)(2,1)S(1)}, bf16[128,2048]{1,0:T(8,128)(2,1)S(1)}, u32[]{:S(2)}, u32[]{:S(2)}) %collective-permute-start.15) | collective-permute-done | bytes 524320 | tf_op jit(solution)/shard_map/ppermute | solution.py:420
  993.3 5.2 collective-permute-start.16
  999.4 3.5 all-to-all-start.1
  1003.0 12.9 %collective-permute-done.16 = bf16[128,2048]{1,0:T(8,128)(2,1)} collective-permute-done((bf16[128,2048]{1,0:T(8,128)(2,1)}, bf16[128,2048]{1,0:T(8,128)(2,1)}, u32[]{:S(2)}, u32[]{:S(2)}) %collective-permute-start.16) | collective-permute-done | bytes 524320 | tf_op jit(solution)/shard_map/ppermute | solution.py:420
  1015.9 2.6 fusion.65
  1019.9 11.3 %convolution_bitcast_fusion = f32[1,512,2048]{2,1,0:T(8,128)} fusion(bf16[2432,512]{1,0:T(8,128)(2,1)} %copy-done.17, bf16[2432,2048]{1,0:T(8,128)(2,1)} %fusion.2), kind=kOutput, calls=%fused_computation.41 | convolution fusion | flops 5100273664 | bytes 16646144 | tf_op jit(solution)/shard_map/dot_general | solution.py:496
  1031.4 5.0 collective-permute-start.17
  1044.3 5.4 collective-permute-done.20
  1049.7 4.7 fusion.55
  (337 shorter events, 108.6 us)
Async XLA Ops:
  7.2 472.6 %copy-start = (bf16[1,512,2048]{2,1,0:T(8,128)(2,1)S(1)}, bf16[1,512,2048]{2,1,0:T(8,128)(2,1)}, u32[]{:S(2)}) copy-start(bf16[1,512,2048]{2,1,0:T(8,128)(2,1)} %param.28) | copy-start | bytes 6291460
  7.2 115.1 %copy-start.18 = (bf16[128,2048]{1,0:T(8,128)(2,1)S(1)}, bf16[128,2048]{1,0:T(8,128)(2,1)}, u32[]{:S(2)}) copy-start(bf16[128,2048]{1,0:T(8,128)(2,1)} %param.16) | copy-start | bytes 1572868
  7.2 182.6 %all-gather.4.cloned.1.call-start = ((), (), s32[]{:S(2)}) async-start(), calls=%async_computation.5 | async-start | bytes 13926400 | tf_op jit(solution)/shard_map/all_gather | solution.py:519
  14.4 205.7 %all-gather.6.cloned.1.call-start = ((), (), s32[]{:S(2)}) async-start(), calls=%async_computation.6 | async-start | bytes 4456448 | tf_op jit(solution)/shard_map/all_gather | solution.py:542
  14.4 21.9 %collective-permute-start.1 = (bf16[128,2048]{1,0:T(8,128)(2,1)}, bf16[128,2048]{1,0:T(8,128)(2,1)S(1)}, u32[]{:S(2)}, u32[]{:S(2)}) collective-permute-start(bf16[128,2048]{1,0:T(8,128)(2,1)} %param.16), channel_id=1, source_target_pairs={{0,8},{2,10},{4,12},{6,14},{8,16},{10,18},{12,20},{14,22},{16,24},... | collective-permute-start | bytes 1572872 | tf_op jit(solution)/shard_map/ppermute | solution.py:420
  19.4 31.0 %collective-permute-start.4 = (bf16[128,2048]{1,0:T(8,128)(2,1)}, bf16[128,2048]{1,0:T(8,128)(2,1)}, u32[]{:S(2)}, u32[]{:S(2)}) collective-permute-start(bf16[128,2048]{1,0:T(8,128)(2,1)} %param.16), channel_id=1, source_target_pairs={{8,0},{10,2},{12,4},{14,6},{16,8},{18,10},{20,12},{22,14},{24,16},... | collective-permute-start | bytes 1572872 | tf_op jit(solution)/shard_map/ppermute | solution.py:420
  36.3 15.4 %collective-permute-start.2 = (bf16[128,2048]{1,0:T(8,128)(2,1)S(1)}, bf16[128,2048]{1,0:T(8,128)(2,1)}, u32[]{:S(2)}, u32[]{:S(2)}) collective-permute-start(bf16[128,2048]{1,0:T(8,128)(2,1)S(1)} %collective-permute-done.1), channel_id=1, source_target_pairs={{8,16},{10,18},{12,20},{14,22},{16,24},{18,26},{20,28},{22,30},{9,... | collective-permute-start | bytes 1572872 | tf_op jit(solution)/shard_map/ppermute | solution.py:420
  50.5 22.1 %collective-permute-start.5 = (bf16[128,2048]{1,0:T(8,128)(2,1)}, bf16[128,2048]{1,0:T(8,128)(2,1)}, u32[]{:S(2)}, u32[]{:S(2)}) collective-permute-start(bf16[128,2048]{1,0:T(8,128)(2,1)} %collective-permute-done.4), channel_id=1, source_target_pairs={{8,0},{10,2},{12,4},{14,6},{16,8},{18,10},{20,12},{22,14},{9,1},{1... | collective-permute-start | bytes 1572872 | tf_op jit(solution)/shard_map/ppermute | solution.py:420
  51.8 22.1 %collective-permute-start.3 = (bf16[128,2048]{1,0:T(8,128)(2,1)}, bf16[128,2048]{1,0:T(8,128)(2,1)}, u32[]{:S(2)}, u32[]{:S(2)}) collective-permute-start(bf16[128,2048]{1,0:T(8,128)(2,1)} %collective-permute-done.2), channel_id=1, source_target_pairs={{16,24},{18,26},{20,28},{22,30},{17,25},{19,27},{21,29},{23,31}} | collective-permute-start | bytes 1572872 | tf_op jit(solution)/shard_map/ppermute | solution.py:420
  53.3 386.6 %all-gather.8.cloned.1.call-start = ((), (), s32[]{:S(2)}) async-start(), calls=%async_computation.7 | async-start | bytes 17301504 | tf_op jit(solution)/shard_map/all_gather | solution.py:590
  72.6 49.6 %collective-permute-start.6 = (bf16[128,2048]{1,0:T(8,128)(2,1)}, bf16[128,2048]{1,0:T(8,128)(2,1)S(1)}, u32[]{:S(2)}, u32[]{:S(2)}) collective-permute-start(bf16[128,2048]{1,0:T(8,128)(2,1)} %collective-permute-done.5), channel_id=1, source_target_pairs={{8,0},{10,2},{12,4},{14,6},{9,1},{11,3},{13,5},{15,7}} | collective-permute-start | bytes 1572872 | tf_op jit(solution)/shard_map/ppermute | solution.py:420
  127.5 57.5 %collective-permute-start.7 = (bf16[4,128,2048]{2,1,0:T(8,128)(2,1)}, bf16[4,128,2048]{2,1,0:T(8,128)(2,1)}, u32[]{:S(2)}, u32[]{:S(2)}) collective-permute-start(bf16[4,128,2048]{2,1,0:T(8,128)(2,1)} %constant_dynamic-slice_fusion.2), channel_id=1, source_target_pairs={{0,4},{2,6},{4,0},{6,2},{8,12},{10,14},{12,8},{14,10},{16,20},{18,... | collective-permute-start | bytes 6291464 | tf_op jit(solution)/shard_map/ppermute | solution.py:414
  132.2 11.6 %collective-permute-start = (bf16[128,2048]{1,0:T(8,128)(2,1)S(1)}, bf16[128,2048]{1,0:T(8,128)(2,1)}, u32[]{:S(2)}, u32[]{:S(2)}) collective-permute-start(bf16[128,2048]{1,0:T(8,128)(2,1)S(1)} %copy-done.10), channel_id=1, source_target_pairs={{0,1},{1,0},{2,3},{3,2},{4,5},{5,4},{6,7},{7,6},{8,9},{9,8},{10,11... | collective-permute-start | bytes 1572872 | tf_op jit(solution)/shard_map/ppermute | solution.py:398
  134.2 78.7 %copy-start.31 = (f32[256,128]{0,1:T(8,128)}, f32[256,128]{0,1:T(8,128)S(1)}, u32[]{:S(2)}) copy-start(f32[256,128]{0,1:T(8,128)S(1)} %get-tuple-element.146) | copy-start | bytes 393220
  134.2 78.7 %copy-start.33 = (f32[256,128]{0,1:T(8,128)}, f32[256,128]{0,1:T(8,128)S(1)}, u32[]{:S(2)}) copy-start(f32[256,128]{0,1:T(8,128)S(1)} %get-tuple-element.145) | copy-start | bytes 393220
  144.9 46.9 %copy-start.21 = (bf16[128,2048]{1,0:T(8,128)(2,1)}, bf16[128,2048]{1,0:T(8,128)(2,1)S(1)}, u32[]{:S(2)}) copy-start(bf16[128,2048]{1,0:T(8,128)(2,1)S(1)} %get-tuple-element.133) | copy-start | bytes 1572868
  145.7 46.2 %copy-start.61 = (f32[256]{0:T(256)}, f32[256]{0:T(256)S(1)}, u32[]{:S(2)}) copy-start(f32[256]{0:T(256)S(1)} %add_rsqrt_fusion) | copy-start | bytes 3076
  191.8 46.4 %copy-start.43 = (f32[2048]{0:T(1024)}, f32[2048]{0:T(1024)S(1)}, u32[]{:S(2)}) copy-start(f32[2048]{0:T(1024)S(1)} %get-tuple-element.82) | copy-start | bytes 24580
  200.3 3.9 collective-permute-start.8
  220.1 17.2 %copy-start.11 = (bf16[128,2048]{1,0:T(8,128)(2,1)S(1)}, bf16[128,2048]{1,0:T(8,128)(2,1)}, u32[]{:S(2)}) copy-start(bf16[128,2048]{1,0:T(8,128)(2,1)} %param.15) | copy-start | bytes 1572868
  223.9 13.5 %collective-permute-start.9 = (bf16[128,2048]{1,0:T(8,128)(2,1)S(1)}, bf16[128,2048]{1,0:T(8,128)(2,1)S(1)}, u32[]{:S(2)}, u32[]{:S(2)}) collective-permute-start(bf16[128,2048]{1,0:T(8,128)(2,1)S(1)} %select_convert_fusion), channel_id=1, source_target_pairs={{0,1},{1,0},{2,3},{3,2},{4,5},{5,4},{6,7},{7,6},{8,9},{9,8},{10,11... | collective-permute-start | bytes 1572872 | tf_op jit(solution)/shard_map/ppermute | solution.py:398
  240.2 496.3 %reduce-scatter.4.cloned.1.call-start = ((), (), s32[]{:S(2)}) async-start(), calls=%async_computation.8 | async-start | bytes 17825792 | tf_op jit(solution)/shard_map/reduce_scatter | solution.py:667
  240.4 131.3 %collective-permute-start.10 = (bf16[4,2,128,2048]{3,2,0,1:T(8,128)(2,1)}, bf16[4,2,128,2048]{3,2,0,1:T(8,128)(2,1)S(1)}, u32[]{:S(2)}, u32[]{:S(2)}) collective-permute-start(bf16[4,2,128,2048]{3,2,0,1:T(8,128)(2,1)} %pad_maximum_fusion.1), channel_id=1, source_target_pairs={{0,1},{1,0},{2,3},{3,2},{4,5},{5,4},{6,7},{7,6},{8,9},{9,8},{10,11... | collective-permute-start | bytes 12582920 | tf_op jit(solution)/shard_map/ppermute | solution.py:398
  390.8 13.5 %collective-permute-start.11 = (bf16[8,256,2048]{2,1,0:T(8,128)(2,1)}, bf16[8,256,2048]{2,1,0:T(8,128)(2,1)}, u32[]{:S(2)}, u32[]{:S(2)}) collective-permute-start(bf16[8,256,2048]{2,1,0:T(8,128)(2,1)} %bitcast.229), channel_id=1, source_target_pairs={{0,2},{2,0},{4,6},{6,4},{8,10},{10,8},{12,14},{14,12},{16,18},{18,... | collective-permute-start | bytes 25165832 | tf_op jit(solution)/shard_map/ppermute | solution.py:414
  394.0 166.6 %copy-start.16 = (pred[8,2,152,256]{3,2,0,1:T(8,128)(4,1)}, pred[8,2,152,256]{3,2,0,1:T(8,128)(4,1)S(1)}, u32[]{:S(2)}) copy-start(pred[8,2,152,256]{3,2,0,1:T(8,128)(4,1)S(1)} %fusion.19) | copy-start | bytes 1867780
  479.8 13.0 %copy-start.17 = (bf16[2432,512]{1,0:T(8,128)(2,1)}, bf16[2432,512]{1,0:T(8,128)(2,1)S(1)}, u32[]{:S(2)}) copy-start(bf16[2432,512]{1,0:T(8,128)(2,1)S(1)} %get-tuple-element.159) | copy-start | bytes 7471108
  513.9 12.8 %copy-start.64 = (bf16[1,2048,512]{2,1,0:T(8,128)(2,1)S(1)}, bf16[1,2048,512]{2,1,0:T(8,128)(2,1)}, u32[]{:S(2)}) copy-start(bf16[1,2048,512]{2,1,0:T(8,128)(2,1)} %param.26) | copy-start | bytes 6291460
  526.7 9.8 copy-start.67
  526.7 9.8 copy-start.69
  560.6 12.5 %copy-start.13 = (bf16[128,2048]{1,0:T(8,128)(2,1)S(1)}, bf16[128,2048]{1,0:T(8,128)(2,1)}, u32[]{:S(2)}) copy-start(bf16[128,2048]{1,0:T(8,128)(2,1)} %multiply_convert_fusion.8) | copy-start | bytes 1572868
  560.6 12.5 %copy-start.46 = (pred[256,16]{0,1:T(8,128)(4,1)S(1)}, pred[256,16]{0,1:T(8,128)(4,1)}, u32[]{:S(2)}) copy-start(pred[256,16]{0,1:T(8,128)(4,1)} %copy-done.45) | copy-start | bytes 12292
  568.2 24.1 %collective-permute-start.12 = (bf16[8,256,2048]{2,1,0:T(8,128)(2,1)}, bf16[8,256,2048]{2,1,0:T(8,128)(2,1)}, u32[]{:S(2)}, u32[]{:S(2)}) collective-permute-start(bf16[8,256,2048]{2,1,0:T(8,128)(2,1)} %multiply_convert_fusion.1), channel_id=1, source_target_pairs={{0,2},{2,0},{4,6},{6,4},{8,10},{10,8},{12,14},{14,12},{16,18},{18,... | collective-permute-start | bytes 25165832 | tf_op jit(solution)/shard_map/ppermute | solution.py:414
  568.8 21.8 %all-to-all-start = ((f32[16,1,256]{2,1,0:T(1,128)}), f32[16,1,256]{2,1,0:T(1,128)S(1)}, u32[]{:S(2)}, u32[]{:S(2)}) async-start(f32[16,1,256]{2,1,0:T(1,128)} %all_to_all.14), calls=%async_computation.1 | async-start | bytes 32768 | tf_op jit(solution)/shard_map/all_to_all | solution.py:640
  572.9 469.5 %reduce-scatter.8.cloned.1.call-start = ((), (), s32[]{:S(2)}) async-start(), calls=%async_computation.10 | async-start | bytes 4456448 | tf_op jit(solution)/shard_map/reduce_scatter | solution.py:707
  590.7 148.5 %collective-permute-start.22 = (f32[128,16]{0,1:T(8,128)S(1)}, f32[128,16]{0,1:T(8,128)S(1)}, u32[]{:S(2)}, u32[]{:S(2)}) collective-permute-start(f32[128,16]{0,1:T(8,128)S(1)} %slice_select_fusion.1), channel_id=1, source_target_pairs={{0,1},{1,0},{2,3},{3,2},{4,5},{5,4},{6,7},{7,6},{8,9},{9,8},{10,11... | collective-permute-start | bytes 24584 | tf_op jit(solution)/shard_map/ppermute | solution.py:398
  592.2 158.9 %copy-start.5 = (f32[128,2048]{1,0:T(8,128)S(1)}, f32[128,2048]{1,0:T(8,128)}, u32[]{:S(2)}) copy-start(f32[128,2048]{1,0:T(8,128)} %copy-done.4) | copy-start | bytes 3145732
  592.2 158.9 %copy-start.44 = (f32[2048]{0:T(1024)S(1)}, f32[2048]{0:T(1024)}, u32[]{:S(2)}) copy-start(f32[2048]{0:T(1024)} %copy-done.43) | copy-start | bytes 24580
  592.2 158.9 %copy-start.60 = (f32[128]{0:T(128)S(1)}, f32[128]{0:T(128)}, u32[]{:S(2)}) copy-start(f32[128]{0:T(128)} %copy-done.59) | copy-start | bytes 1540
  604.3 148.9 %copy-start.19 = (bf16[128,2048]{1,0:T(8,128)(2,1)S(1)}, bf16[128,2048]{1,0:T(8,128)(2,1)}, u32[]{:S(2)}) copy-start(bf16[128,2048]{1,0:T(8,128)(2,1)} %param.16) | copy-start | bytes 1572868
  737.7 13.4 %collective-permute-start.21 = (bf16[128,2048]{1,0:T(8,128)(2,1)S(1)}, bf16[128,2048]{1,0:T(8,128)(2,1)S(1)}, u32[]{:S(2)}, u32[]{:S(2)}) collective-permute-start(bf16[128,2048]{1,0:T(8,128)(2,1)S(1)} %broadcast_select_fusion.7), channel_id=1, source_target_pairs={{0,1},{1,0},{2,3},{3,2},{4,5},{5,4},{6,7},{7,6},{8,9},{9,8},{10,11... | collective-permute-start | bytes 1572872 | tf_op jit(solution)/shard_map/ppermute | solution.py:398
  739.3 26.9 %copy-start.36 = (bf16[8,128,256]{2,1,0:T(8,128)(2,1)S(1)}, bf16[8,128,256]{2,1,0:T(8,128)(2,1)}, u32[]{:S(2)}) copy-start(bf16[8,128,256]{2,1,0:T(8,128)(2,1)} %copy-done.35) | copy-start | bytes 1572868
  753.1 16.4 %copy-start.20 = (f32[128,2048]{1,0:T(8,128)}, f32[128,2048]{1,0:T(8,128)S(1)}, u32[]{:S(2)}) copy-start(f32[128,2048]{1,0:T(8,128)S(1)} %get-tuple-element.167) | copy-start | bytes 3145732
  753.5 12.5 %collective-permute-start.23 = (bf16[128,2048]{1,0:T(8,128)(2,1)S(1)}, bf16[128,2048]{1,0:T(8,128)(2,1)S(1)}, u32[]{:S(2)}, u32[]{:S(2)}) collective-permute-start(bf16[128,2048]{1,0:T(8,128)(2,1)S(1)} %fusion.124), channel_id=1, source_target_pairs={{0,1},{1,0},{2,3},{3,2},{4,5},{5,4},{6,7},{7,6},{8,9},{9,8},{10,11... | collective-permute-start | bytes 1572872 | tf_op jit(solution)/shard_map/ppermute | solution.py:398
  769.5 284.9 %reduce-scatter.6.cloned.1.call-start = ((), (), s32[]{:S(2)}) async-start(), calls=%async_computation.9 | async-start | bytes 13369344 | tf_op jit(solution)/shard_map/reduce_scatter | solution.py:750
  786.2 4.9 collective-permute-start.24
  806.3 90.6 %collective-permute-start.13 = (bf16[8,128,2048]{2,1,0:T(8,128)(2,1)}, bf16[8,128,2048]{2,1,0:T(8,128)(2,1)}, u32[]{:S(2)}, u32[]{:S(2)}) collective-permute-start(bf16[8,128,2048]{2,1,0:T(8,128)(2,1)} %dynamic-slice_bitcast_fusion), channel_id=1, source_target_pairs={{0,1},{1,0},{2,3},{3,2},{4,5},{5,4},{6,7},{7,6},{8,9},{9,8},{10,11... | collective-permute-start | bytes 12582920 | tf_op jit(solution)/shard_map/ppermute | solution.py:398
  818.7 86.8 %slice-start = ((s8[9961472]{0:T(1024)(128)(4,1)}), s8[4194304]{0:T(1024)(128)(4,1)S(1)}, s32[]{:S(2)}) async-start(s8[9961472]{0:T(1024)(128)(4,1)} %bitcast.236), calls=%async_computation.11 | async-start | bytes 8388608
  818.7 86.8 %slice-start.1 = ((s8[9961472]{0:T(1024)(128)(4,1)}), s8[4194304]{0:T(1024)(128)(4,1)S(1)}, s32[]{:S(2)}) async-start(s8[9961472]{0:T(1024)(128)(4,1)} %bitcast.236), calls=%async_computation.12 | async-start | bytes 8388608
  832.6 72.9 %slice-start.2 = ((s8[9961472]{0:T(1024)(128)(4,1)}), s8[1572864]{0:T(1024)(128)(4,1)S(1)}, s32[]{:S(2)}) async-start(s8[9961472]{0:T(1024)(128)(4,1)} %bitcast.236), calls=%async_computation.13 | async-start | bytes 3145728
  902.4 10.8 %copy-start.6 = (bf16[8,128,2048]{2,1,0:T(8,128)(2,1)}, bf16[8,128,2048]{2,1,0:T(8,128)(2,1)S(1)}, u32[]{:S(2)}) copy-start(bf16[8,128,2048]{2,1,0:T(8,128)(2,1)S(1)} %fusion.7) | copy-start | bytes 12582916
  903.9 10.8 %copy-start.38 = (bf16[256,1024]{1,0:T(8,128)(2,1)S(1)}, bf16[256,1024]{1,0:T(8,128)(2,1)}, u32[]{:S(2)}) copy-start(bf16[256,1024]{1,0:T(8,128)(2,1)} %copy-done.37) | copy-start | bytes 1572868
  903.9 61.6 %collective-permute-start.14 = (bf16[4,128,2048]{2,1,0:T(8,128)(2,1)}, bf16[4,128,2048]{2,1,0:T(8,128)(2,1)}, u32[]{:S(2)}, u32[]{:S(2)}) collective-permute-start(bf16[4,128,2048]{2,1,0:T(8,128)(2,1)} %dynamic-slice_bitcast_fusion.1), channel_id=1, source_target_pairs={{0,4},{2,6},{4,0},{6,2},{8,12},{10,14},{12,8},{14,10},{16,20},{18,... | collective-permute-start | bytes 6291464 | tf_op jit(solution)/shard_map/ppermute | solution.py:414
  914.7 50.8 %copy-start.7 = (bf16[8,128,2048]{2,1,0:T(8,128)(2,1)S(1)}, bf16[8,128,2048]{2,1,0:T(8,128)(2,1)}, u32[]{:S(2)}) copy-start(bf16[8,128,2048]{2,1,0:T(8,128)(2,1)} %copy-done.6) | copy-start | bytes 12582916
  923.4 47.5 %copy-start.12 = (bf16[128,2048]{1,0:T(8,128)(2,1)S(1)}, bf16[128,2048]{1,0:T(8,128)(2,1)}, u32[]{:S(2)}) copy-start(bf16[128,2048]{1,0:T(8,128)(2,1)} %param.15) | copy-start | bytes 1572868
  923.4 47.4 %collective-permute-start.25 = (bf16[128,2048]{1,0:T(8,128)(2,1)S(1)}, bf16[128,2048]{1,0:T(8,128)(2,1)S(1)}, u32[]{:S(2)}, u32[]{:S(2)}) collective-permute-start(bf16[128,2048]{1,0:T(8,128)(2,1)S(1)} %broadcast_select_fusion.3), channel_id=1, source_target_pairs={{0,1},{1,0},{2,3},{3,2},{4,5},{5,4},{6,7},{7,6},{8,9},{9,8},{10,11... | collective-permute-start | bytes 1572872 | tf_op jit(solution)/shard_map/ppermute | solution.py:398
  967.9 68.5 %copy-start.8 = (bf16[4,128,2048]{2,1,0:T(8,128)(2,1)}, bf16[4,128,2048]{2,1,0:T(8,128)(2,1)S(1)}, u32[]{:S(2)}) copy-start(bf16[4,128,2048]{2,1,0:T(8,128)(2,1)S(1)} %fusion.12) | copy-start | bytes 6291460
  968.9 23.5 %collective-permute-start.15 = (bf16[128,2048]{1,0:T(8,128)(2,1)S(1)}, bf16[128,2048]{1,0:T(8,128)(2,1)S(1)}, u32[]{:S(2)}, u32[]{:S(2)}) collective-permute-start(bf16[128,2048]{1,0:T(8,128)(2,1)S(1)} %get-tuple-element.119), channel_id=1, source_target_pairs={{0,8},{2,10},{4,12},{6,14},{1,9},{3,11},{5,13},{7,15}} | collective-permute-start | bytes 1572872 | tf_op jit(solution)/shard_map/ppermute | solution.py:420
  972.2 26.3 %collective-permute-start.26 = (f32[16,2304]{1,0:T(8,128)S(1)}, f32[16,2304]{1,0:T(8,128)S(1)}, u32[]{:S(2)}, u32[]{:S(2)}) collective-permute-start(f32[16,2304]{1,0:T(8,128)S(1)} %pad_maximum_fusion.9), channel_id=1, source_target_pairs={{0,1},{1,0},{2,3},{3,2},{4,5},{5,4},{6,7},{7,6},{8,9},{9,8},{10,11... | collective-permute-start | bytes 442376 | tf_op jit(solution)/shard_map/ppermute | solution.py:398
  972.6 30.3 %collective-permute-start.18 = (bf16[128,2048]{1,0:T(8,128)(2,1)}, bf16[128,2048]{1,0:T(8,128)(2,1)}, u32[]{:S(2)}, u32[]{:S(2)}) collective-permute-start(bf16[128,2048]{1,0:T(8,128)(2,1)} %get-tuple-element.120), channel_id=1, source_target_pairs={{24,16},{26,18},{28,20},{30,22},{25,17},{27,19},{29,21},{31,23}} | collective-permute-start | bytes 1572872 | tf_op jit(solution)/shard_map/ppermute | solution.py:420
  993.3 22.6 %collective-permute-start.16 = (bf16[128,2048]{1,0:T(8,128)(2,1)}, bf16[128,2048]{1,0:T(8,128)(2,1)}, u32[]{:S(2)}, u32[]{:S(2)}) collective-permute-start(bf16[128,2048]{1,0:T(8,128)(2,1)} %fusion.64), channel_id=1, source_target_pairs={{0,8},{2,10},{4,12},{6,14},{8,16},{10,18},{12,20},{14,22},{1,9},{3... | collective-permute-start | bytes 1572872 | tf_op jit(solution)/shard_map/ppermute | solution.py:420
  999.4 31.8 %all-to-all-start.1 = ((f32[16,1,2432]{2,1,0:T(1,128)}), f32[16,1,2432]{2,1,0:T(1,128)S(1)}, u32[]{:S(2)}, u32[]{:S(2)}) async-start(f32[16,1,2432]{2,1,0:T(1,128)} %copy.201), calls=%async_computation.4 | async-start | bytes 311296 | tf_op jit(solution)/shard_map/all_to_all | solution.py:777
  1018.4 17.9 %collective-permute-start.19 = (bf16[128,2048]{1,0:T(8,128)(2,1)}, bf16[128,2048]{1,0:T(8,128)(2,1)}, u32[]{:S(2)}, u32[]{:S(2)}) collective-permute-start(bf16[128,2048]{1,0:T(8,128)(2,1)} %get-tuple-element.118), channel_id=1, source_target_pairs={{16,8},{18,10},{20,12},{22,14},{24,16},{26,18},{28,20},{30,22},{17... | collective-permute-start | bytes 1572872 | tf_op jit(solution)/shard_map/ppermute | solution.py:420
  1031.4 13.0 %collective-permute-start.17 = (bf16[128,2048]{1,0:T(8,128)(2,1)}, bf16[128,2048]{1,0:T(8,128)(2,1)}, u32[]{:S(2)}, u32[]{:S(2)}) collective-permute-start(bf16[128,2048]{1,0:T(8,128)(2,1)} %get-tuple-element.117), channel_id=1, source_target_pairs={{0,8},{2,10},{4,12},{6,14},{8,16},{10,18},{12,20},{14,22},{16,24},... | collective-permute-start | bytes 1572872 | tf_op jit(solution)/shard_map/ppermute | solution.py:420
  1038.3 11.4 %collective-permute-start.20 = (bf16[128,2048]{1,0:T(8,128)(2,1)}, bf16[128,2048]{1,0:T(8,128)(2,1)}, u32[]{:S(2)}, u32[]{:S(2)}) collective-permute-start(bf16[128,2048]{1,0:T(8,128)(2,1)} %fusion.63), channel_id=1, source_target_pairs={{8,0},{10,2},{12,4},{14,6},{16,8},{18,10},{20,12},{22,14},{24,16},... | collective-permute-start | bytes 1572872 | tf_op jit(solution)/shard_map/ppermute | solution.py:420
  (45 other events, 178.5 us)
Sparse Core Ops, SparseCore 0:
  14.5 126.0 all-gather.3
  142.7 56.5 all-gather.5
  240.3 146.4 all-gather.7
  560.7 175.7 reduce-scatter.3
  769.6 72.9 reduce-scatter.7
  846.6 168.0 reduce-scatter.5
